TPU v7x, 32 devices: a whole 2x2x4 slice. The times are simulated.
32 devices in a mesh: dp: 8 (over z, y), chan: 4 (over x, core).
Axes of the slice: x: 2, y: 2, z: 4, core: 2. Of those that a mesh axis runs over, the one named last changes fastest.
Arguments:
- activations: bfloat16 [8, 16, 64, 1024], P('dp', None, None, 'chan'), may hold values from -60 to 60
- cotangent: bfloat16 [8, 16, 64, 1024], P('dp', None, None, 'chan'), may hold values from -6 to 6
- dw_kernel: float32 [49, 1024], P(None, 'chan'), may hold values from -0.875 to 0.875
- norm_gain: float32 [4, 1024], P(None, 'chan'), may hold values from 0.1 to 1.9
- norm_bias: float32 [4, 1024], P(None, 'chan'), may hold values from -3 to 3
- w_in: bfloat16 [1024, 4096], P(None, 'chan'), may hold values from -0.1875 to 0.1875
- b_in: float32 [4096], P('chan'), may hold values from -3 to 3
- w_out: bfloat16 [4096, 1024], P('chan'), may hold values from -0.09375 to 0.09375
- layer_scale: float32 [1024], P('chan'), may hold values from 0.3 to 1.5
- group_sizes: int32 [4], replicated, may hold values from 1 to 4, 8 in all
Outputs:
- result: bfloat16 [8, 16, 64, 1024], P('dp', None, None, 'chan')
- d_input: bfloat16 [8, 16, 64, 1024], P('dp', None, None, 'chan')
- d_kernel: float32 [49, 1024], P(None, 'chan')
- d_gain: float32 [4, 1024], P(None, 'chan')
- d_bias: float32 [4, 1024], P(None, 'chan')
- d_w_in: float32 [1024, 4096], P('dp', 'chan')
- d_b_in: float32 [4096], P('chan')
- d_w_out: float32 [4096, 1024], P('chan', 'dp')
- d_scale: float32 [1024], P('chan')
Inputs may be any that keep to these rules, and one draw needn't show every extreme that they name: `group_sizes`: the sizes sum to 8, each is at least one, and the largest is exactly 4.
All inputs are finite; a program needn't handle non-finite values.
Results may differ from a plain program's by a relative error of at most 0.015.
Values may be sent and summed in bfloat16 or wider, within the bound.
A program may use at most 128 MiB of HBM per device.

v0:
```python
import jax
import jax.numpy as jnp
from jax import lax
from jax.sharding import PartitionSpec as P

KS = 7


EPS = 1e-05


def depthwise(field, kernel):
    reach = KS // 2
    height, width = (field.shape[1], field.shape[2])
    padded = jnp.pad(field, ((0, 0), (reach, reach), (reach, reach), (0, 0)))
    running = jnp.zeros(field.shape, jnp.float32)
    for shift_row in range(KS):
        for shift_col in range(KS):
            window = padded[:, shift_row : shift_row + height, shift_col : shift_col + width, :]
            running = running + window * kernel[shift_row * KS + shift_col]
    return running


def kernel_grad(field, upstream):
    reach = KS // 2
    height, width = (field.shape[1], field.shape[2])
    padded = jnp.pad(field, ((0, 0), (reach, reach), (reach, reach), (0, 0)))
    collected = []
    for shift_row in range(KS):
        for shift_col in range(KS):
            window = padded[:, shift_row : shift_row + height, shift_col : shift_col + width, :]
            collected.append(jnp.sum(window * upstream, axis=(0, 1, 2)))
    return jnp.stack(collected)


def group_owners(group_sizes, number):
    group_ends = jnp.cumsum(group_sizes)
    positions = jnp.arange(number, dtype=jnp.int32)
    labels = jnp.sum((group_ends[None, :] <= positions[:, None]).astype(jnp.int32), axis=1)
    return (jnp.arange(group_sizes.shape[0], dtype=jnp.int32)[:, None] == labels[None, :]).astype(
        jnp.float32
    )


def body(
    activations,
    cotangent,
    dw_kernel,
    norm_gain,
    norm_bias,
    w_in,
    b_in,
    w_out,
    layer_scale,
    group_sizes,
):
    height, width, channels = (activations.shape[1], activations.shape[2], activations.shape[3])
    row_count = height * width
    devices = lax.axis_size("dp")
    position = lax.axis_index("dp")
    group_ends = jnp.cumsum(group_sizes)
    own_group = jnp.sum((group_ends <= position).astype(jnp.int32))
    member = (jnp.arange(group_sizes.shape[0], dtype=jnp.int32) == own_group).astype(jnp.float32)
    counts = group_sizes.astype(jnp.float32) * row_count
    own_count = jnp.sum(member * counts)
    source = activations.astype(jnp.float32)
    filtered = depthwise(source, dw_kernel).reshape(row_count, channels)
    moments = jnp.stack([jnp.sum(filtered, axis=0), jnp.sum(filtered * filtered, axis=0)])
    per_device = lax.all_gather(moments[None], "dp", axis=0, tiled=True)
    owners = group_owners(group_sizes, devices)
    totals = jnp.sum(owners[:, :, None, None] * per_device[None], axis=1)
    group_mean = totals[:, 0] / counts[:, None]
    group_var = totals[:, 1] / counts[:, None] - group_mean * group_mean
    group_rstd = lax.rsqrt(group_var + EPS)
    own_mean = jnp.sum(member[:, None] * group_mean, axis=0)
    own_rstd = jnp.sum(member[:, None] * group_rstd, axis=0)
    own_gain = jnp.sum(member[:, None] * norm_gain, axis=0)
    own_bias = jnp.sum(member[:, None] * norm_bias, axis=0)
    centered = (filtered - own_mean) * own_rstd
    normed = (centered * own_gain + own_bias).astype(jnp.bfloat16)
    gathered = lax.all_gather(normed, "chan", axis=1, tiled=True)
    hidden = jnp.dot(gathered, w_in, preferred_element_type=jnp.float32) + b_in
    activated = jax.nn.gelu(hidden).astype(jnp.bfloat16)
    partial_branch = jnp.dot(activated, w_out, preferred_element_type=jnp.float32)
    branch = lax.psum_scatter(
        partial_branch.astype(jnp.bfloat16), "chan", scatter_dimension=1, tiled=True
    ).astype(jnp.float32)
    initial = source.reshape(row_count, channels)
    result = (initial + layer_scale * branch).astype(jnp.bfloat16).reshape(activations.shape)
    incoming = cotangent.reshape(row_count, channels).astype(jnp.float32)
    scale_local = jnp.sum(incoming * branch, axis=0)
    d_branch = (incoming * layer_scale).astype(jnp.bfloat16)
    branch_full = lax.all_gather(d_branch, "chan", axis=1, tiled=True)
    contract_rows = (((0,), (0,)), ((), ()))
    contract_cols = (((1,), (1,)), ((), ()))
    out_local_t = lax.dot_general(
        branch_full, activated, contract_rows, preferred_element_type=jnp.float32
    )
    d_activated = lax.dot_general(
        branch_full, w_out, contract_cols, preferred_element_type=jnp.float32
    )
    _, pullback = jax.vjp(jax.nn.gelu, hidden)
    d_hidden = pullback(d_activated)[0]
    bias_local = jnp.sum(d_hidden, axis=0)
    hidden_b = d_hidden.astype(jnp.bfloat16)
    in_local = lax.dot_general(
        gathered, hidden_b, contract_rows, preferred_element_type=jnp.float32
    )
    hidden_cols = in_local.shape[1]
    both_local = jnp.concatenate([in_local, out_local_t], axis=1)
    both_sums = lax.psum_scatter(
        both_local.astype(jnp.bfloat16), "dp", scatter_dimension=0, tiled=True
    ).astype(jnp.float32)
    d_w_in = both_sums[:, :hidden_cols]
    d_w_out = both_sums[:, hidden_cols:].T
    partial_normed = lax.dot_general(
        hidden_b, w_in, contract_cols, preferred_element_type=jnp.float32
    )
    d_normed = lax.psum_scatter(
        partial_normed.astype(jnp.bfloat16), "chan", scatter_dimension=1, tiled=True
    ).astype(jnp.float32)
    grad_moments = jnp.stack([jnp.sum(d_normed * centered, axis=0), jnp.sum(d_normed, axis=0)])
    grad_rows = lax.all_gather(grad_moments[None], "dp", axis=0, tiled=True)
    grad_owners = group_owners(group_sizes, devices)
    grad_totals = jnp.sum(grad_owners[:, :, None, None] * grad_rows[None], axis=1)
    d_gain = grad_totals[:, 0]
    d_bias = grad_totals[:, 1]
    own_dgain = jnp.sum(member[:, None] * d_gain, axis=0)
    own_dbias = jnp.sum(member[:, None] * d_bias, axis=0)
    d_filtered = (
        own_gain * own_rstd * (d_normed - own_dbias / own_count - centered * own_dgain / own_count)
    )
    d_filtered = d_filtered.reshape(activations.shape)
    kernel_local = kernel_grad(source, d_filtered)
    d_kernel, d_b_in, d_scale = lax.psum((kernel_local, bias_local, scale_local), "dp")
    d_input = (cotangent.astype(jnp.float32) + depthwise(d_filtered, dw_kernel[::-1])).astype(
        jnp.bfloat16
    )
    return (result, d_input, d_kernel, d_gain, d_bias, d_w_in, d_b_in, d_w_out, d_scale)


def solution(mesh):
    in_specs = (
        P("dp", None, None, "chan"),
        P("dp", None, None, "chan"),
        P(None, "chan"),
        P(None, "chan"),
        P(None, "chan"),
        P(None, "chan"),
        P("chan"),
        P("chan", None),
        P("chan"),
        P(),
    )
    out_specs = (
        P("dp", None, None, "chan"),
        P("dp", None, None, "chan"),
        P(None, "chan"),
        P(None, "chan"),
        P(None, "chan"),
        P("dp", "chan"),
        P("chan"),
        P("chan", "dp"),
        P("chan"),
    )
    return jax.shard_map(body, mesh=mesh, in_specs=in_specs, out_specs=out_specs, check_vma=False)
```

profile of v0, /device:TPU:0, one launch (start us, length us, event | category | flops | bytes accessed | tf_op | source)
XLA Modules:
  0.0 303.6 jit_solution(11111486553160216814)
XLA Ops:
  7.2 0.0 copy-start
  7.2 0.0 copy-start.5
  7.2 0.0 copy-start.4
  7.2 0.0 all-gather.7.cloned.1.call-start
  7.3 1.0 reduce-window.8
  8.2 0.6 fusion.117
  8.9 0.6 compare_convert_fusion.1
  9.5 1.9 fusion.116
  11.4 0.9 fusion.124
  12.4 1.1 fusion.122
  13.4 1.1 fusion.123
  14.6 0.1 convert_reduce_fusion.1
  14.7 1.1 convert_element_type.75
  15.8 9.7 %fusion.118 = (f32[256]{0:T(256)S(1)}, f32[256]{0:T(256)S(1)}, f32[1,16,64,256]{3,2,1,0:T(8,128)}) fusion(f32[256]{0:T(256)S(1)} %bitcast.229, f32[256]{0:T(256)S(1)} %bitcast.231, f32[256]{0:T(256)S(1)} %bitcast.235, f32[256]{0:T(256)S(1)} %bitcast.237, f32[256]{0:T(256)S(1)} %bitcast.239, f32[256]{0:T(256)S(1)} %bitcast.241, f32[256]{0:T(256)S(1)} %bitcast.243, ...), kind=kLoop, calls=%fused_computation.304 | loop fusion | flops 26213888 | bytes 2149376 | tf_op jit(solution)/shard_map/reduce_sum | solution.py:68
  25.5 27.9 %all-gather.2 = f32[8,2,256]{2,1,0:T(2,128)S(1)} all-gather(f32[1,2,256]{2,1,0:T(2,128)S(1)} %maximum_bitcast_fusion), channel_id=2, replica_groups=mesh['dp'=8,'chan'=4] {'dp'}, dimensions={0}, use_global_device_ids=true | all-gather | bytes 18432 | tf_op jit(solution)/shard_map/all_gather | solution.py:69
  53.5 0.1 multiply_reduce_fusion.51
  53.6 0.0 copy-done.5
  53.6 0.0 copy-done.4
  53.6 0.1 multiply_reduce_fusion.57
  53.7 2.2 add_convert_fusion
  55.9 0.0 all-gather.7.cloned.1.call-update
  55.9 0.0 copy-start.9
  55.9 0.0 reduce-scatter.6.cloned.1.call-start
  56.0 22.3 %all-gather.7.cloned.1.call-done = bf16[1024,1024]{1,0:T(8,128)(2,1)} async-done(((bf16[1024,256]{1,0:T(8,128)(2,1)}), bf16[1024,1024]{1,0:T(8,128)(2,1)}) %all-gather.7.cloned.1.call-update) | async-done | bytes 2097168 | tf_op jit(solution)/shard_map/all_gather | solution.py:81
  78.3 4.6 %fusion.127 = f32[1024,1024]{1,0:T(8,128)S(1)} fusion(bf16[1024,1024]{1,0:T(8,128)(2,1)} %all-gather.7.cloned.1.call-done, bf16[1024,1024]{1,0:T(8,128)(2,1)} %param.15), kind=kOutput, calls=%fused_computation.311 | convolution fusion | flops 2147483648 | bytes 8388608 | tf_op jit(solution)/shard_map/dot_general | solution.py:82
  82.8 0.0 copy-start.10
  82.8 1.9 copy-done.10
  84.8 0.0 copy-done
  84.8 4.2 %convolution_convert_fusion.3 = bf16[1024,1024]{1,0:T(8,128)(2,1)} fusion(bf16[1024,1024]{1,0:T(8,128)(2,1)S(1)} %copy-done, f32[1024,1024]{1,0:T(8,128)S(1)} %fusion.127, f32[1024]{0:T(1024)S(1)} %copy-done.9), kind=kOutput, calls=%fused_computation.109 | convolution fusion | flops 2159017984 | bytes 8392704 | tf_op jit(solution)/shard_map/dot_general | solution.py:84
  88.9 0.0 reduce-scatter.6.cloned.1.call-update
  89.0 0.0 all-gather.9.cloned.1.call-start
  89.0 31.3 %reduce-scatter.6.cloned.1.call-done = bf16[1024,256]{1,0:T(8,128)(2,1)} async-done(((bf16[1024,1024]{1,0:T(8,128)(2,1)}), bf16[1024,256]{1,0:T(8,128)(2,1)}) %reduce-scatter.6.cloned.1.call-update) | async-done | bytes 524304 | tf_op jit(solution)/shard_map/reduce_scatter | solution.py:85
  120.3 2.7 fusion.8
  122.9 0.0 all-gather.9.cloned.1.call-update
  123.0 0.2 reduce-scatter.8.cloned.1.call-start
  123.2 22.7 %all-gather.9.cloned.1.call-done = bf16[1024,1024]{1,0:T(8,128)(2,1)} async-done(((bf16[1024,256]{1,0:T(8,128)(2,1)}), bf16[1024,1024]{1,0:T(8,128)(2,1)}) %all-gather.9.cloned.1.call-update) | async-done | bytes 2097168 | tf_op jit(solution)/shard_map/all_gather | solution.py:93
  145.9 7.5 %fusion.119 = (f32[1024]{0:T(1024)S(1)}, bf16[1024,1024]{1,0:T(8,128)(2,1)S(1)}) fusion(f32[1024,1024]{1,0:T(8,128)} %copy-done.10, f32[1024]{0:T(1024)S(1)} %copy-done.9, bf16[1024,1024]{1,0:T(8,128)(2,1)} %all-gather.9.cloned.1.call-done, bf16[1024,1024]{1,0:T(8,128)(2,1)S(1)} %copy-done), kind=kOutput, calls=%fused_computation.305 | convolution fusion | flops 2170551296 | bytes 10493952 | tf_op jit(solution)/shard_map/dot_general | solution.py:99
  153.4 1.3 copy-done.12
  154.7 3.8 %convolution_convert_fusion.2 = bf16[1024,1024]{1,0:T(8,128)(2,1)} fusion(bf16[1024,1024]{1,0:T(8,128)(2,1)S(1)} %copy-done.7, bf16[1024,1024]{1,0:T(8,128)(2,1)S(1)} %get-tuple-element.99), kind=kOutput, calls=%fused_computation.108 | convolution fusion | flops 2148532224 | bytes 6291456 | tf_op jit(solution)/shard_map/dot_general | solution.py:116
  158.5 0.0 reduce-scatter.8.cloned.1.call-update
  158.5 0.0 reduce-scatter.10.cloned.1.call-start
  158.6 4.8 %convolution_convert_fusion.1 = bf16[1024,1024]{0,1:T(8,128)(2,1)S(1)} fusion(bf16[1024,1024]{1,0:T(8,128)(2,1)} %all-gather.7.cloned.1.call-done, bf16[1024,1024]{1,0:T(8,128)(2,1)} %copy-done.12), kind=kOutput, calls=%fused_computation.107 | convolution fusion | flops 2148532224 | bytes 6291456 | tf_op jit(solution)/shard_map/dot_general | solution.py:106
  163.4 3.0 convolution_convert_fusion
  166.4 2.4 pad_maximum_fusion
  168.8 6.5 %copy.27 = bf16[1024,2048]{1,0:T(8,128)(2,1)} copy(bf16[1024,2048]{0,1:T(8,128)(2,1)} %pad_maximum_fusion) | data formatting | bytes 8388608
  175.3 0.0 reduce-scatter.10.cloned.1.call-update
  175.3 14.5 %reduce-scatter.8.cloned.1.call-done = bf16[1024,256]{1,0:T(8,128)(2,1)} async-done(((bf16[1024,1024]{1,0:T(8,128)(2,1)}), bf16[1024,256]{1,0:T(8,128)(2,1)}) %reduce-scatter.8.cloned.1.call-update) | async-done | bytes 524304 | tf_op jit(solution)/shard_map/reduce_scatter | solution.py:119
  189.8 1.7 fusion.9
  191.5 0.0 copy-start.3
  191.6 27.2 %all-gather.3 = f32[8,2,256]{2,1,0:T(2,128)S(1)} all-gather(f32[1,2,256]{2,1,0:T(2,128)S(1)} %maximum_bitcast_fusion.1), channel_id=3, replica_groups=mesh['dp'=8,'chan'=4] {'dp'}, dimensions={0}, use_global_device_ids=true | all-gather | bytes 18432 | tf_op jit(solution)/shard_map/all_gather | solution.py:123
  218.8 0.1 multiply_reduce_fusion.50
  218.9 0.6 multiply_reduce_fusion.53
  219.5 0.7 broadcast_divide_fusion
  220.2 4.5 %multiply_reduce_fusion.1 = (f32[256]{0:T(256)S(1)}, f32[256]{0:T(256)S(1)}, f32[256]{0:T(256)S(1)}, f32[256]{0:T(256)S(1)}, f32[256]{0:T(256)S(1)}, /*index=5*/...) fusion(f32[1,16,64,256]{3,2,1,0:T(8,128)S(1)} %convert_element_, ...), kind=kLoop, calls=%fused_computation.224 | loop fusion | flops 11529728 | bytes 3693572 | tf_op jit(solution)/shard_map/reduce_sum | solution.py:32
  224.7 1.6 multiply_reduce_fusion.2
  226.3 2.3 multiply_reduce_fusion
  228.6 0.2 stack.223
  228.8 36.8 %all-reduce.2 = (f32[49,256]{1,0:T(8,128)}, f32[1024]{0:T(1024)}, f32[256]{0:T(256)}) all-reduce(f32[49,256]{1,0:T(8,128)S(1)} %stack.223, f32[1024]{0:T(1024)S(1)} %get-tuple-element.98, f32[256]{0:T(256)S(1)} %get-tuple-element.104), channel_id=1, replica_groups=mesh['dp'=8,'chan'=4] {'dp'}, use_global_device_ids=true, to_apply=%region_67.68 | all-reduce | flops 13824 | bytes 110592 | tf_op jit(solution)/shard_map/psum | solution.py:135
  265.6 26.2 %fusion.106 = bf16[1,16,64,256]{3,2,1,0:T(8,128)(2,1)} fusion(f32[1,16,64,256]{3,2,1,0:T(8,128)} %bitcast.209, bf16[1,16,64,256]{3,2,1,0:T(8,128)(2,1)} %param.11, f32[256]{0:T(256)S(1)} %bitcast.230, f32[256]{0:T(256)S(1)} %bitcast.232, f32[256]{0:T(256)S(1)} %bitcast.236, f32[256]{0:T(256)S(1)} %bitcast.238, f32[256]{0:T(256)S(1)} %bitcast.240, ...), kind=kLoop, calls=%fused_computation.215 | loop fusion | flops 26214400 | bytes 2147328 | tf_op jit(solution)/shard_map/convert_element_type | solution.py:136
  291.8 0.0 reduce-scatter.10.cloned.1.call-done
  291.8 1.3 copy.28
  293.2 1.1 convert_element_type.94
  294.2 1.0 copy.26
  295.2 1.9 slice_bitcast_fusion
  (24 shorter events, 0.1 us)
Async XLA Ops:
  7.2 77.6 %copy-start = (bf16[1024,1024]{1,0:T(8,128)(2,1)S(1)}, bf16[1024,1024]{1,0:T(8,128)(2,1)}, u32[]{:S(2)}) copy-start(bf16[1024,1024]{1,0:T(8,128)(2,1)} %param.17) | copy-start | bytes 6291460
  7.2 46.4 %copy-start.5 = (f32[4,256]{1,0:T(4,128)S(1)}, f32[4,256]{1,0:T(4,128)}, u32[]{:S(2)}) copy-start(f32[4,256]{1,0:T(4,128)} %param.14) | copy-start | bytes 12292
  7.2 46.4 %copy-start.4 = (f32[4,256]{1,0:T(4,128)S(1)}, f32[4,256]{1,0:T(4,128)}, u32[]{:S(2)}) copy-start(f32[4,256]{1,0:T(4,128)} %param.13) | copy-start | bytes 12292
  7.2 71.1 %all-gather.7.cloned.1.call-start = ((), (), s32[]{:S(2)}) async-start(), calls=%async_computation.3 | async-start | bytes 2621440 | tf_op jit(solution)/shard_map/all_gather | solution.py:81
  55.9 28.9 %copy-start.9 = (f32[1024]{0:T(1024)S(1)}, f32[1024]{0:T(1024)}, u32[]{:S(2)}) copy-start(f32[1024]{0:T(1024)} %param.16) | copy-start | bytes 12292
  55.9 64.4 %reduce-scatter.6.cloned.1.call-start = ((), (), s32[]{:S(2)}) async-start(), calls=%async_computation.4 | async-start | bytes 2621440 | tf_op jit(solution)/shard_map/reduce_scatter | solution.py:85
  82.8 1.9 copy-start.10
  88.9 31.3 %copy-start.6 = (f32[256]{0:T(256)S(1)}, f32[256]{0:T(256)}, u32[]{:S(2)}) copy-start(f32[256]{0:T(256)} %param.18) | copy-start | bytes 3076
  89.0 57.0 %all-gather.9.cloned.1.call-start = ((), (), s32[]{:S(2)}) async-start(), calls=%async_computation.5 | async-start | bytes 2621440 | tf_op jit(solution)/shard_map/all_gather | solution.py:93
  123.0 66.9 %reduce-scatter.8.cloned.1.call-start = ((), (), s32[]{:S(2)}) async-start(), calls=%async_computation.6 | async-start | bytes 2621440 | tf_op jit(solution)/shard_map/reduce_scatter | solution.py:119
  145.9 8.8 %copy-start.7 = (bf16[1024,1024]{1,0:T(8,128)(2,1)S(1)}, bf16[1024,1024]{1,0:T(8,128)(2,1)}, u32[]{:S(2)}) copy-start(bf16[1024,1024]{1,0:T(8,128)(2,1)} %param.15) | copy-start | bytes 6291460
  153.4 1.3 copy-start.12
  158.5 133.3 %reduce-scatter.10.cloned.1.call-start = ((), (), s32[]{:S(2)}) async-start(), calls=%async_computation.7 | async-start | bytes 4718592
  158.6 4.8 %copy-start.8 = (bf16[1024,1024]{1,0:T(8,128)(2,1)S(1)}, bf16[1024,1024]{1,0:T(8,128)(2,1)}, u32[]{:S(2)}) copy-start(bf16[1024,1024]{1,0:T(8,128)(2,1)} %all-gather.9.cloned.1.call-done) | copy-start | bytes 6291460
  158.6 4.8 %copy-start.11 = (f32[1024,1024]{1,0:T(8,128)S(1)}, f32[1024,1024]{1,0:T(8,128)}, u32[]{:S(2)}) copy-start(f32[1024,1024]{1,0:T(8,128)} %copy-done.10) | copy-start | bytes 12582916
  189.8 30.3 %copy-start.1 = (f32[1,16,64,256]{3,2,1,0:T(8,128)S(1)}, f32[1,16,64,256]{3,2,1,0:T(8,128)}, u32[]{:S(2)}) copy-start(f32[1,16,64,256]{3,2,1,0:T(8,128)} %get-tuple-element.103) | copy-start | bytes 3145732
  191.5 33.1 %copy-start.3 = (bf16[1,16,64,256]{3,2,1,0:T(8,128)(2,1)S(1)}, bf16[1,16,64,256]{3,2,1,0:T(8,128)(2,1)}, u32[]{:S(2)}) copy-start(bf16[1,16,64,256]{3,2,1,0:T(8,128)(2,1)} %param.10) | copy-start | bytes 1572868
  224.6 3.9 %copy-start.2 = (f32[1024,256]{1,0:T(8,128)}, f32[1024,256]{1,0:T(8,128)S(1)}, u32[]{:S(2)}) copy-start(f32[1024,256]{1,0:T(8,128)S(1)} %get-tuple-element.100) | copy-start | bytes 3145732
Sparse Core Ops, SparseCore 0:
  56.0 22.2 all-gather.6
  89.1 31.1 reduce-scatter.5
  123.1 22.8 all-gather.8
  158.6 31.1 reduce-scatter.7
  193.3 89.9 reduce-scatter.9
where the time goes:
time: 304 us
  blocking collectives  91.9 us (30%)
  waiting for transfers between devices  90.9 us (30%)
  other arithmetic  61.3 us (20%)
  matrix products  27.7 us (9%)
  local copies, waits for them, and re-layouts  17.3 us (6%)
  between operations  14.1 us (5%)
    psum x1, blocking collectives, body(): lax.psum((kernel_local, bias_local, scale_local), 'dp')  36.8 us
    reduce_scatter x1, waiting for transfers between devices, body(): lax.psum_scatter(partial_branch.astype(jnp.bfloat16), 'chan', scatter_dim...  31.3 us
    all_gather x1, blocking collectives, body(): per_device = lax.all_gather(moments[None], 'dp', axis=0, tiled=True)  27.9 us
    all_gather x1, blocking collectives, body(): grad_rows = lax.all_gather(grad_moments[None], 'dp', axis=0, tiled=True)  27.2 us
    convert_element_type x1, other arithmetic, body(): (cotangent.astype(jnp.float32) + depthwise(d_filtered, dw_kernel[::-1]))....  26.2 us
    all_gather x1, waiting for transfers between devices, body(): branch_full = lax.all_gather(d_branch, 'chan', axis=1, tiled=True)  22.7 us
    all_gather x1, waiting for transfers between devices, body(): gathered = lax.all_gather(normed, 'chan', axis=1, tiled=True)  22.3 us
    reduce_scatter x1, waiting for transfers between devices, body(): lax.psum_scatter(partial_normed.astype(jnp.bfloat16), 'chan', scatter_dim...  14.5 us
  transfers between devices with their start and end apart: 5, of which 4 were waited for; matrix products, arithmetic and copies ran while one was open for 18% of the time, Pallas kernels for 0%

commit v1 on v0

--- a/solution.py
+++ b/solution.py
@@ -1,6 +1,10 @@
+import functools
+
 import jax
 import jax.numpy as jnp
 from jax import lax
+from jax.experimental import pallas as pl
+from jax.experimental.pallas import tpu as pltpu
 from jax.sharding import PartitionSpec as P
 
 KS = 7
@@ -9,28 +13,133 @@
 EPS = 1e-05
 
 
-def depthwise(field, kernel):
-    reach = KS // 2
-    height, width = (field.shape[1], field.shape[2])
-    padded = jnp.pad(field, ((0, 0), (reach, reach), (reach, reach), (0, 0)))
-    running = jnp.zeros(field.shape, jnp.float32)
-    for shift_row in range(KS):
-        for shift_col in range(KS):
-            window = padded[:, shift_row : shift_row + height, shift_col : shift_col + width, :]
-            running = running + window * kernel[shift_row * KS + shift_col]
-    return running
-
-
-def kernel_grad(field, upstream):
-    reach = KS // 2
-    height, width = (field.shape[1], field.shape[2])
-    padded = jnp.pad(field, ((0, 0), (reach, reach), (reach, reach), (0, 0)))
-    collected = []
-    for shift_row in range(KS):
-        for shift_col in range(KS):
-            window = padded[:, shift_row : shift_row + height, shift_col : shift_col + width, :]
-            collected.append(jnp.sum(window * upstream, axis=(0, 1, 2)))
-    return jnp.stack(collected)
+REACH = KS // 2
+SUB = 8
+LANE = 128
+
+
+def fill_shifts(rows, width, load_row, shifts_ref):
+    def one(r, carry):
+        value = load_row(r)
+        column = lax.broadcasted_iota(jnp.int32, value.shape, 0)
+        for c in range(KS):
+            off = c - REACH
+            if off == 0:
+                shifts_ref[c, r] = value
+            else:
+                moved = pltpu.roll(value, (-off) % width, 0)
+                keep = (column + off >= 0) & (column + off < width)
+                shifts_ref[c, r] = jnp.where(keep, moved, 0.0)
+        return carry
+
+    lax.fori_loop(0, rows, one, 0)
+
+
+def conv_forward(rows, width, channels, shifts_ref, kernel_ref, out_ref, moments_ref):
+    for lb in range(channels // LANE):
+        lanes = slice(lb * LANE, (lb + 1) * LANE)
+
+        def block(sb, carry):
+            first, second = carry
+            cols = pl.ds(pl.multiple_of(sb * SUB, SUB), SUB)
+            acc = [None] * rows
+            for c in range(KS):
+                taps = [kernel_ref[a * KS + c : a * KS + c + 1, lanes] for a in range(KS)]
+                for r_in in range(rows):
+                    value = shifts_ref[c, r_in, cols, lanes]
+                    for a in range(KS):
+                        r = r_in - a + REACH
+                        if 0 <= r < rows:
+                            term = value * taps[a]
+                            acc[r] = term if acc[r] is None else acc[r] + term
+            for r in range(rows):
+                out_ref[r, cols, lanes] = acc[r]
+                first = first + acc[r]
+                second = second + acc[r] * acc[r]
+            return first, second
+
+        zero = jnp.zeros((SUB, LANE), jnp.float32)
+        first, second = lax.fori_loop(0, width // SUB, block, (zero, zero))
+        moments_ref[0:1, lanes] = jnp.sum(first, axis=0, keepdims=True)
+        moments_ref[1:2, lanes] = jnp.sum(second, axis=0, keepdims=True)
+
+
+def conv_backward(rows, width, channels, shifts_ref, source_ref, kernel_ref, grad_ref, taps_ref):
+    for lb in range(channels // LANE):
+        lanes = slice(lb * LANE, (lb + 1) * LANE)
+        taps_ref[:, :, lanes] = jnp.zeros((KS * KS, SUB, LANE), jnp.float32)
+
+        def block(sb, carry):
+            cols = pl.ds(pl.multiple_of(sb * SUB, SUB), SUB)
+            acc = [None] * rows
+            xs = [source_ref[r, cols, lanes] for r in range(rows)]
+            for c in range(KS):
+                b = KS - 1 - c
+                taps = [
+                    kernel_ref[(KS - 1 - a) * KS + b : (KS - 1 - a) * KS + b + 1, lanes]
+                    for a in range(KS)
+                ]
+                sums = [None] * KS
+                for r_in in range(rows):
+                    value = shifts_ref[c, r_in, cols, lanes]
+                    for a in range(KS):
+                        r = r_in - a + REACH
+                        if 0 <= r < rows:
+                            term = value * taps[a]
+                            acc[r] = term if acc[r] is None else acc[r] + term
+                        x_row = r_in + a - REACH
+                        if 0 <= x_row < rows:
+                            term = value * xs[x_row]
+                            sums[a] = term if sums[a] is None else sums[a] + term
+                for a in range(KS):
+                    taps_ref[a * KS + b, :, lanes] += sums[a]
+            for r in range(rows):
+                grad_ref[r, cols, lanes] = acc[r]
+            return carry
+
+        lax.fori_loop(0, width // SUB, block, 0)
+
+
+def forward_kernel(x_ref, kernel_ref, out_ref, moments_ref, shifts_ref):
+    _, rows, width, channels = x_ref.shape
+    fill_shifts(rows, width, lambda r: x_ref[0, r].astype(jnp.float32), shifts_ref)
+    conv_forward(rows, width, channels, shifts_ref, kernel_ref, out_ref, moments_ref)
+
+
+def backward_kernel(
+    x_ref, cot_ref, kernel_ref, dn_ref, filt_ref, stat_ref, din_ref, dk_ref,
+    shifts_ref, source_ref, grad_ref, taps_ref
+):
+    _, rows, width, channels = x_ref.shape
+
+    def convert(r, carry):
+        source_ref[r] = x_ref[0, r].astype(jnp.float32)
+        return carry
+
+    lax.fori_loop(0, rows, convert, 0)
+    mean, rstd, scale = stat_ref[0:1], stat_ref[1:2], stat_ref[2:3]
+    mean_bias, mean_gain = stat_ref[3:4], stat_ref[4:5]
+
+    def load_row(r):
+        centered = (filt_ref[r] - mean) * rstd
+        return scale * (dn_ref[r].astype(jnp.float32) - mean_bias - centered * mean_gain)
+
+    fill_shifts(rows, width, load_row, shifts_ref)
+    conv_backward(
+        rows, width, channels, shifts_ref, source_ref, kernel_ref, grad_ref, taps_ref
+    )
+    for tap in range(KS * KS):
+        dk_ref[tap : tap + 1] = jnp.sum(taps_ref[tap], axis=0, keepdims=True)
+
+    def finish(r, carry):
+        din_ref[0, r] = (cot_ref[0, r].astype(jnp.float32) + grad_ref[r]).astype(jnp.bfloat16)
+        return carry
+
+    lax.fori_loop(0, rows, finish, 0)
+
+
+VMEM = pl.BlockSpec(memory_space=pltpu.VMEM)
+PARAMS = pltpu.CompilerParams(vmem_limit_bytes=50 * 1024 * 1024)
 
 
 def group_owners(group_sizes, number):
@@ -64,8 +173,18 @@
     counts = group_sizes.astype(jnp.float32) * row_count
     own_count = jnp.sum(member * counts)
     source = activations.astype(jnp.float32)
-    filtered = depthwise(source, dw_kernel).reshape(row_count, channels)
-    moments = jnp.stack([jnp.sum(filtered, axis=0), jnp.sum(filtered * filtered, axis=0)])
+    filtered_image, moments = pl.pallas_call(
+        forward_kernel,
+        out_shape=(
+            jax.ShapeDtypeStruct((height, width, channels), jnp.float32),
+            jax.ShapeDtypeStruct((2, channels), jnp.float32),
+        ),
+        in_specs=[VMEM] * 2,
+        out_specs=(VMEM, VMEM),
+        scratch_shapes=[pltpu.VMEM((KS, height, width, channels), jnp.float32)],
+        compiler_params=PARAMS,
+    )(activations, dw_kernel)
+    filtered = filtered_image.reshape(row_count, channels)
     per_device = lax.all_gather(moments[None], "dp", axis=0, tiled=True)
     owners = group_owners(group_sizes, devices)
     totals = jnp.sum(owners[:, :, None, None] * per_device[None], axis=1)
@@ -127,15 +246,33 @@
     d_bias = grad_totals[:, 1]
     own_dgain = jnp.sum(member[:, None] * d_gain, axis=0)
     own_dbias = jnp.sum(member[:, None] * d_bias, axis=0)
-    d_filtered = (
-        own_gain * own_rstd * (d_normed - own_dbias / own_count - centered * own_dgain / own_count)
-    )
-    d_filtered = d_filtered.reshape(activations.shape)
-    kernel_local = kernel_grad(source, d_filtered)
+    stats = jnp.stack(
+        [own_mean, own_rstd, own_gain * own_rstd, own_dbias / own_count, own_dgain / own_count]
+    )
+    d_input, kernel_local = pl.pallas_call(
+        backward_kernel,
+        out_shape=(
+            jax.ShapeDtypeStruct(activations.shape, jnp.bfloat16),
+            jax.ShapeDtypeStruct((KS * KS, channels), jnp.float32),
+        ),
+        in_specs=[VMEM] * 6,
+        out_specs=(VMEM, VMEM),
+        scratch_shapes=[
+            pltpu.VMEM((KS, height, width, channels), jnp.float32),
+            pltpu.VMEM((height, width, channels), jnp.float32),
+            pltpu.VMEM((height, width, channels), jnp.float32),
+            pltpu.VMEM((KS * KS, SUB, channels), jnp.float32),
+        ],
+        compiler_params=PARAMS,
+    )(
+        activations,
+        cotangent,
+        dw_kernel,
+        d_normed.reshape(height, width, channels),
+        filtered_image,
+        stats,
+    )
     d_kernel, d_b_in, d_scale = lax.psum((kernel_local, bias_local, scale_local), "dp")
-    d_input = (cotangent.astype(jnp.float32) + depthwise(d_filtered, dw_kernel[::-1])).astype(
-        jnp.bfloat16
-    )
     return (result, d_input, d_kernel, d_gain, d_bias, d_w_in, d_b_in, d_w_out, d_scale)
 
 

time: 304 us -> 287 us (0.944)
  other arithmetic: 61.3 us -> 17.1 us
  Pallas kernels: 0 us -> 13.5 us
  waiting for transfers between devices: 90.9 us -> 102 us
    convert_element_type x2 -> x0, other arithmetic: 27.4 us -> none  [the longest x1 26.2 us: body(): (cotangent.astype(jnp.float32) + depthwise(d_filtered, dw_kernel[::-1]))....]
    reduce_sum x5 -> x1, other arithmetic: 18.7 us -> 0.61 us  [body(): own_dgain = jnp.sum(member[:, None] * d_gain, axis=0)]
    pallas_call x0 -> x2, Pallas kernels: none -> 13.5 us  [the longest x1 9.36 us: body(): pl.pallas_call(backward_kernel, out_shape=(jax.ShapeDtypeStruct(activatio...]
    unnamed x6, waiting for transfers between devices: 0.1 us -> 11.6 us
    unnamed x29 -> x31, local copies, waits for them, and re-layouts: 12.1 us -> 17.2 us
    slice x4 -> x1, local copies, waits for them, and re-layouts: 3.13 us -> 0.01 us  [body(): d_gain = grad_totals[:, 0]]
  transfers between devices with their start and end apart: 5 -> 5, of which waited for: 4 -> 5; matrix products, arithmetic and copies ran while one was open for 18% -> 8% of each run, Pallas kernels for 0% -> 3%
where the time goes in v1:
time: 287 us; the launch traced here: 286 us
  waiting for transfers between devices  102 us (36%)
  blocking collectives  92 us (32%)
  matrix products  27.7 us (10%)
  local copies, waits for them, and re-layouts  19.2 us (7%)
  other arithmetic  17.1 us (6%)
  between operations  14 us (5%)
  Pallas kernels  13.5 us (5%)
    psum x1, blocking collectives, body(): lax.psum((kernel_local, bias_local, scale_local), 'dp')  37 us
    reduce_scatter x1, waiting for transfers between devices, body(): lax.psum_scatter(partial_branch.astype(jnp.bfloat16), 'chan', scatter_dim...  31.3 us
    all_gather x1, blocking collectives, body(): per_device = lax.all_gather(moments[None], 'dp', axis=0, tiled=True)  27.9 us
    all_gather x1, blocking collectives, body(): grad_rows = lax.all_gather(grad_moments[None], 'dp', axis=0, tiled=True)  27 us
    all_gather x1, waiting for transfers between devices, body(): branch_full = lax.all_gather(d_branch, 'chan', axis=1, tiled=True)  22.9 us
    all_gather x1, waiting for transfers between devices, body(): gathered = lax.all_gather(normed, 'chan', axis=1, tiled=True)  22.3 us
    unnamed x31, local copies, waits for them, and re-layouts  17.2 us
    reduce_scatter x1, waiting for transfers between devices, body(): lax.psum_scatter(partial_normed.astype(jnp.bfloat16), 'chan', scatter_dim...  14.3 us
  transfers between devices with their start and end apart: 5, of which 5 were waited for; matrix products, arithmetic and copies ran while one was open for 8% of the time, Pallas kernels for 3%

profile of v1, /device:TPU:0, one launch (start us, length us, event | category | flops | bytes accessed | tf_op | source)
XLA Modules:
  0.0 286.3 jit_solution(2393791494990474852)
XLA Ops:
  7.2 0.0 copy-start
  7.2 0.0 all-gather.7.cloned.1.call-start
  7.2 1.0 reduce-window.8
  8.2 0.6 fusion.16
  8.8 0.6 compare_convert_fusion.1
  9.5 1.9 fusion.15
  11.4 0.1 convert_reduce_fusion.1
  11.5 1.0 copy-done.1
  12.5 0.8 copy-done.5
  13.4 4.1 %shard_map.169 = (f32[16,64,256]{2,1,0:T(8,128)S(1)}, f32[2,256]{1,0:T(2,128)S(1)}) custom-call(bf16[1,16,64,256]{3,2,1,0:T(8,128)(2,1)S(1)} %copy-done.1, f32[49,256]{1,0:T(8,128)S(1)} %copy-done.5), custom_call_target="tpu_custom_call" | custom-call | tf_op jit(solution)/shard_map/pallas_call | solution.py:176
  17.5 27.9 %all-gather.2 = f32[8,2,256]{2,1,0:T(2,128)S(1)} all-gather(f32[1,2,256]{2,1,0:T(2,128)S(1)} %bitcast.62), channel_id=2, replica_groups=mesh['dp'=8,'chan'=4] {'dp'}, dimensions={0}, use_global_device_ids=true | all-gather | bytes 18432 | tf_op jit(solution)/shard_map/all_gather | solution.py:188
  45.4 0.1 multiply_reduce_fusion.2
  45.5 0.8 multiply_reduce_fusion.8
  46.3 1.0 add_convert_fusion
  47.3 0.0 all-gather.7.cloned.1.call-update
  47.3 0.0 copy-start.10
  47.3 0.0 reduce-scatter.6.cloned.1.call-start
  47.4 22.3 %all-gather.7.cloned.1.call-done = bf16[1024,1024]{1,0:T(8,128)(2,1)} async-done(((bf16[1024,256]{1,0:T(8,128)(2,1)}), bf16[1024,1024]{1,0:T(8,128)(2,1)}) %all-gather.7.cloned.1.call-update) | async-done | bytes 2097168 | tf_op jit(solution)/shard_map/all_gather | solution.py:200
  69.7 4.5 %fusion.21 = f32[1024,1024]{1,0:T(8,128)S(1)} fusion(bf16[1024,1024]{1,0:T(8,128)(2,1)} %all-gather.7.cloned.1.call-done, bf16[1024,1024]{1,0:T(8,128)(2,1)} %param.15), kind=kOutput, calls=%fused_computation.58 | convolution fusion | flops 2147483648 | bytes 8388608 | tf_op jit(solution)/shard_map/dot_general | solution.py:201
  74.3 0.0 copy-start.11
  74.3 1.9 copy-done.11
  76.2 0.0 copy-done
  76.2 0.0 copy-done.10
  76.2 4.2 %convolution_convert_fusion.3 = bf16[1024,1024]{1,0:T(8,128)(2,1)} fusion(bf16[1024,1024]{1,0:T(8,128)(2,1)S(1)} %copy-done, f32[1024,1024]{1,0:T(8,128)S(1)} %fusion.21, f32[1024]{0:T(1024)S(1)} %copy-done.10), kind=kOutput, calls=%fused_computation.13 | convolution fusion | flops 2159017984 | bytes 8392704 | tf_op jit(solution)/shard_map/dot_general | solution.py:203
  80.4 0.0 reduce-scatter.6.cloned.1.call-update
  80.4 0.0 all-gather.9.cloned.1.call-start
  80.4 31.3 %reduce-scatter.6.cloned.1.call-done = bf16[1024,256]{1,0:T(8,128)(2,1)} async-done(((bf16[1024,1024]{1,0:T(8,128)(2,1)}), bf16[1024,256]{1,0:T(8,128)(2,1)}) %reduce-scatter.6.cloned.1.call-update) | async-done | bytes 524304 | tf_op jit(solution)/shard_map/reduce_scatter | solution.py:204
  111.7 0.0 copy-done.7
  111.7 2.6 fusion.9
  114.4 0.0 all-gather.9.cloned.1.call-update
  114.4 0.0 reduce-scatter.8.cloned.1.call-start
  114.4 22.9 %all-gather.9.cloned.1.call-done = bf16[1024,1024]{1,0:T(8,128)(2,1)} async-done(((bf16[1024,256]{1,0:T(8,128)(2,1)}), bf16[1024,1024]{1,0:T(8,128)(2,1)}) %all-gather.9.cloned.1.call-update) | async-done | bytes 2097168 | tf_op jit(solution)/shard_map/all_gather | solution.py:212
  137.3 7.5 %fusion.17 = (f32[1024]{0:T(1024)S(1)}, bf16[1024,1024]{1,0:T(8,128)(2,1)S(1)}) fusion(f32[1024,1024]{1,0:T(8,128)} %copy-done.11, f32[1024]{0:T(1024)S(1)} %copy-done.10, bf16[1024,1024]{1,0:T(8,128)(2,1)} %all-gather.9.cloned.1.call-done, bf16[1024,1024]{1,0:T(8,128)(2,1)S(1)} %copy-done), kind=kOutput, calls=%fused_computation.55 | convolution fusion | flops 2170551296 | bytes 10493952 | tf_op jit(solution)/shard_map/dot_general | solution.py:218
  144.8 0.0 copy-start.13
  144.8 1.3 copy-done.13
  146.1 0.0 copy-done.8
  146.1 3.8 %convolution_convert_fusion.2 = bf16[1024,1024]{1,0:T(8,128)(2,1)} fusion(bf16[1024,1024]{1,0:T(8,128)(2,1)S(1)} %copy-done.8, bf16[1024,1024]{1,0:T(8,128)(2,1)S(1)} %get-tuple-element.56), kind=kOutput, calls=%fused_computation.12 | convolution fusion | flops 2148532224 | bytes 6291456 | tf_op jit(solution)/shard_map/dot_general | solution.py:235
  149.9 0.0 reduce-scatter.8.cloned.1.call-update
  149.9 0.2 reduce-scatter.10.cloned.1.call-start
  150.2 4.8 %convolution_convert_fusion.1 = bf16[1024,1024]{0,1:T(8,128)(2,1)S(1)} fusion(bf16[1024,1024]{1,0:T(8,128)(2,1)} %all-gather.7.cloned.1.call-done, bf16[1024,1024]{1,0:T(8,128)(2,1)} %copy-done.13), kind=kOutput, calls=%fused_computation.11 | convolution fusion | flops 2148532224 | bytes 6291456 | tf_op jit(solution)/shard_map/dot_general | solution.py:225
  154.9 0.0 copy-done.9
  155.0 0.0 copy-done.12
  155.0 3.0 %convolution_convert_fusion = bf16[1024,1024]{0,1:T(8,128)(2,1)S(1)} fusion(bf16[1024,1024]{1,0:T(8,128)(2,1)S(1)} %copy-done.9, f32[1024,1024]{1,0:T(8,128)S(1)} %copy-done.12, f32[1024]{0:T(1024)S(1)} %copy-done.10), kind=kOutput, calls=%fused_computation.10 | convolution fusion | flops 2159017984 | bytes 8392704 | tf_op jit(solution)/shard_map/dot_general | solution.py:215
  158.0 2.4 pad_maximum_fusion
  160.4 6.5 %copy.27 = bf16[1024,2048]{1,0:T(8,128)(2,1)} copy(bf16[1024,2048]{0,1:T(8,128)(2,1)} %pad_maximum_fusion) | data formatting | bytes 8388608
  166.9 0.0 reduce-scatter.10.cloned.1.call-update
  166.9 14.3 %reduce-scatter.8.cloned.1.call-done = bf16[1024,256]{1,0:T(8,128)(2,1)} async-done(((bf16[1024,1024]{1,0:T(8,128)(2,1)}), bf16[1024,256]{1,0:T(8,128)(2,1)}) %reduce-scatter.8.cloned.1.call-update) | async-done | bytes 524304 | tf_op jit(solution)/shard_map/reduce_scatter | solution.py:238
  181.2 1.4 multiply_reduce_fusion
  182.6 27.0 %all-gather.3 = f32[8,2,256]{2,1,0:T(2,128)S(1)} all-gather(f32[1,2,256]{2,1,0:T(2,128)S(1)} %maximum_bitcast_fusion), channel_id=3, replica_groups=mesh['dp'=8,'chan'=4] {'dp'}, dimensions={0}, use_global_device_ids=true | all-gather | bytes 18432 | tf_op jit(solution)/shard_map/all_gather | solution.py:242
  209.6 2.2 convert.21.dn_ref
  211.8 0.1 multiply_reduce_fusion.1
  211.9 0.6 multiply_reduce_fusion.3
  212.5 0.7 broadcast_divide_fusion
  213.2 0.0 copy-start.2
  213.2 1.0 copy-done.2
  214.3 1.2 copy-done.3
  215.5 1.0 copy-done.4
  216.5 9.4 %shard_map.170 = (bf16[1,16,64,256]{3,2,1,0:T(8,128)(2,1)}, f32[49,256]{1,0:T(8,128)S(1)}) custom-call(bf16[1,16,64,256]{3,2,1,0:T(8,128)(2,1)S(1)} %copy-done.2, bf16[1,16,64,256]{3,2,1,0:T(8,128)(2,1)S(1)} %copy-done.4, f32[49,256]{1,0:T(8,128)S(1)} %copy-done.6, f32[16,64,256]{2,1,0:T(8,128)S(1)} %copy-done.3, ...), custom_call_target="tpu_custom_call" | custom-call | tf_op jit(solution)/shard_map/pallas_call | solution.py:252
  225.9 37.0 %all-reduce = (f32[49,256]{1,0:T(8,128)}, f32[1024]{0:T(1024)}, f32[256]{0:T(256)}) all-reduce(f32[49,256]{1,0:T(8,128)S(1)} %get-tuple-element.16, f32[1024]{0:T(1024)S(1)} %get-tuple-element.55, f32[256]{0:T(256)S(1)} %get-tuple-element.59), channel_id=1, replica_groups=mesh['dp'=8,'chan'=4] {'dp'}, use_global_device_ids=true, to_apply=%region_16.17 | all-reduce | flops 13824 | bytes 110592 | tf_op jit(solution)/shard_map/psum | solution.py:275
  262.9 11.5 %reduce-scatter.10.cloned.1.call-done = bf16[128,2048]{1,0:T(8,128)(2,1)} async-done(((bf16[1024,2048]{1,0:T(8,128)(2,1)}), bf16[128,2048]{1,0:T(8,128)(2,1)}) %reduce-scatter.10.cloned.1.call-update) | async-done | bytes 524304
  274.5 1.3 copy.28
  275.8 1.1 convert_element_type.79
  276.9 1.0 copy.26
  277.9 1.9 slice_bitcast_fusion
  (19 shorter events, 0.1 us)
Async XLA Ops:
  7.2 69.0 %copy-start = (bf16[1024,1024]{1,0:T(8,128)(2,1)S(1)}, bf16[1024,1024]{1,0:T(8,128)(2,1)}, u32[]{:S(2)}) copy-start(bf16[1024,1024]{1,0:T(8,128)(2,1)} %param.17) | copy-start | bytes 6291460
  7.2 62.5 %all-gather.7.cloned.1.call-start = ((), (), s32[]{:S(2)}) async-start(), calls=%async_computation.3 | async-start | bytes 2621440 | tf_op jit(solution)/shard_map/all_gather | solution.py:200
  11.5 1.0 copy-start.1
  12.5 0.8 copy-start.5
  47.3 28.9 %copy-start.10 = (f32[1024]{0:T(1024)S(1)}, f32[1024]{0:T(1024)}, u32[]{:S(2)}) copy-start(f32[1024]{0:T(1024)} %param.16) | copy-start | bytes 12292
  47.3 64.4 %reduce-scatter.6.cloned.1.call-start = ((), (), s32[]{:S(2)}) async-start(), calls=%async_computation.4 | async-start | bytes 2621440 | tf_op jit(solution)/shard_map/reduce_scatter | solution.py:204
  74.3 1.9 copy-start.11
  76.2 35.5 %copy-start.7 = (f32[256]{0:T(256)S(1)}, f32[256]{0:T(256)}, u32[]{:S(2)}) copy-start(f32[256]{0:T(256)} %param.18) | copy-start | bytes 3076
  80.4 57.0 %all-gather.9.cloned.1.call-start = ((), (), s32[]{:S(2)}) async-start(), calls=%async_computation.5 | async-start | bytes 2621440 | tf_op jit(solution)/shard_map/all_gather | solution.py:212
  114.4 66.9 %reduce-scatter.8.cloned.1.call-start = ((), (), s32[]{:S(2)}) async-start(), calls=%async_computation.6 | async-start | bytes 2621440 | tf_op jit(solution)/shard_map/reduce_scatter | solution.py:238
  137.3 8.8 %copy-start.8 = (bf16[1024,1024]{1,0:T(8,128)(2,1)S(1)}, bf16[1024,1024]{1,0:T(8,128)(2,1)}, u32[]{:S(2)}) copy-start(bf16[1024,1024]{1,0:T(8,128)(2,1)} %param.15) | copy-start | bytes 6291460
  144.8 1.3 copy-start.13
  149.9 124.6 %reduce-scatter.10.cloned.1.call-start = ((), (), s32[]{:S(2)}) async-start(), calls=%async_computation.7 | async-start | bytes 4718592
  150.2 4.8 %copy-start.9 = (bf16[1024,1024]{1,0:T(8,128)(2,1)S(1)}, bf16[1024,1024]{1,0:T(8,128)(2,1)}, u32[]{:S(2)}) copy-start(bf16[1024,1024]{1,0:T(8,128)(2,1)} %all-gather.9.cloned.1.call-done) | copy-start | bytes 6291460
  150.2 4.8 %copy-start.12 = (f32[1024,1024]{1,0:T(8,128)S(1)}, f32[1024,1024]{1,0:T(8,128)}, u32[]{:S(2)}) copy-start(f32[1024,1024]{1,0:T(8,128)} %copy-done.11) | copy-start | bytes 12582916
  166.9 46.3 %copy-start.6 = (f32[49,256]{1,0:T(8,128)S(1)}, f32[49,256]{1,0:T(8,128)}, u32[]{:S(2)}) copy-start(f32[49,256]{1,0:T(8,128)} %kernel_ref.3) | copy-start | bytes 150532
  213.2 1.1 copy-start.2
  214.3 1.2 copy-start.3
  215.5 1.0 copy-start.4
Sparse Core Ops, SparseCore 0:
  47.5 22.2 all-gather.6
  80.5 31.1 reduce-scatter.5
  114.5 22.8 all-gather.8
  150.1 31.1 reduce-scatter.7
  184.7 89.7 reduce-scatter.9

commit v2 on v1

v2 whole, which is shorter than its diff:
```python
import functools

import jax
import jax.numpy as jnp
from jax import lax
from jax.experimental import pallas as pl
from jax.experimental.pallas import tpu as pltpu
from jax.sharding import PartitionSpec as P

KS = 7


EPS = 1e-05


REACH = KS // 2
SUB = 8
LANE = 128


def fill_shifts(rows, width, load_row, shifts_ref):
    def one(r, carry):
        value = load_row(r)
        column = lax.broadcasted_iota(jnp.int32, value.shape, 0)
        for c in range(KS):
            off = c - REACH
            if off == 0:
                shifts_ref[c, r] = value
            else:
                moved = pltpu.roll(value, (-off) % width, 0)
                keep = (column + off >= 0) & (column + off < width)
                shifts_ref[c, r] = jnp.where(keep, moved, 0.0)
        return carry

    lax.fori_loop(0, rows, one, 0)


def conv_forward(rows, width, channels, shifts_ref, kernel_ref, out_ref, moments_ref):
    for lb in range(channels // LANE):
        lanes = slice(lb * LANE, (lb + 1) * LANE)

        def block(sb, carry):
            first, second = carry
            cols = pl.ds(pl.multiple_of(sb * SUB, SUB), SUB)
            acc = [None] * rows
            for c in range(KS):
                taps = [kernel_ref[a * KS + c : a * KS + c + 1, lanes] for a in range(KS)]
                for r_in in range(rows):
                    value = shifts_ref[c, r_in, cols, lanes]
                    for a in range(KS):
                        r = r_in - a + REACH
                        if 0 <= r < rows:
                            term = value * taps[a]
                            acc[r] = term if acc[r] is None else acc[r] + term
            for r in range(rows):
                out_ref[r, cols, lanes] = acc[r]
                first = first + acc[r]
                second = second + acc[r] * acc[r]
            return first, second

        zero = jnp.zeros((SUB, LANE), jnp.float32)
        first, second = lax.fori_loop(0, width // SUB, block, (zero, zero))
        moments_ref[0:1, lanes] = jnp.sum(first, axis=0, keepdims=True)
        moments_ref[1:2, lanes] = jnp.sum(second, axis=0, keepdims=True)


def conv_backward(rows, width, channels, shifts_ref, source_ref, kernel_ref, grad_ref, taps_ref):
    for lb in range(channels // LANE):
        lanes = slice(lb * LANE, (lb + 1) * LANE)
        taps_ref[:, :, lanes] = jnp.zeros((KS * KS, SUB, LANE), jnp.float32)

        def block(sb, carry):
            cols = pl.ds(pl.multiple_of(sb * SUB, SUB), SUB)
            acc = [None] * rows
            xs = [source_ref[r, cols, lanes] for r in range(rows)]
            for c in range(KS):
                b = KS - 1 - c
                taps = [
                    kernel_ref[(KS - 1 - a) * KS + b : (KS - 1 - a) * KS + b + 1, lanes]
                    for a in range(KS)
                ]
                sums = [None] * KS
                for r_in in range(rows):
                    value = shifts_ref[c, r_in, cols, lanes]
                    for a in range(KS):
                        r = r_in - a + REACH
                        if 0 <= r < rows:
                            term = value * taps[a]
                            acc[r] = term if acc[r] is None else acc[r] + term
                        x_row = r_in + a - REACH
                        if 0 <= x_row < rows:
                            term = value * xs[x_row]
                            sums[a] = term if sums[a] is None else sums[a] + term
                for a in range(KS):
                    taps_ref[a * KS + b, :, lanes] += sums[a]
            for r in range(rows):
                grad_ref[r, cols, lanes] = acc[r]
            return carry

        lax.fori_loop(0, width // SUB, block, 0)


MESH = pl.DeviceIdType.MESH
F32 = jnp.float32
BF16 = jnp.bfloat16
CONTRACT_ROWS = (((0,), (0,)), ((), ()))
CONTRACT_COLS = (((1,), (1,)), ((), ()))
GELU_SCALE = 0.7978845608028654
GELU_CUBE = 0.044715


def gelu_and_slope(h):
    square = h * h
    t = jnp.tanh(GELU_SCALE * (h + GELU_CUBE * (square * h)))
    half = 0.5 * (1.0 + t)
    slope = half + (0.5 * h) * (1.0 - t * t) * (
        GELU_SCALE * (1.0 + (3.0 * GELU_CUBE) * square)
    )
    return h * half, slope


def block_kernel(
    n_dp, n_y, n_chan, chunks,
    sizes_ref, x_hbm, cot_hbm, taps_in, gain_ref, bias_ref, w_in_hbm, b_in_ref, w_out_hbm, scale_ref,
    result_ref, din_ref, dk_ref, dgain_ref, dbias_ref, dwin_ref, dbin_ref, dwout_ref, dscale_ref,
    x_ref, cot_ref, w_in, w_out, source, filt, shifts, tap_sums,
    gath, dfull, d_act, act, hid_b,
    sib_send, sib_recv, own_part, x_send, x_recv, dn,
    mom_send, mom_recv, w_send, w_recv, z_send, z_recv,
    pack_y, pack_z, bias_acc,
    in_sems, ag_xs, ag_xr, ag_ss, ag_sr, ag_fs, ag_fr,
    rs_ss, rs_sr, rs_xs, rs_xr, mom_ss, mom_sr, wy_s, wy_r, wz_s, wz_r, py_s, py_r, pz_s, pz_r,
):
    images, height, width, channels = x_ref.shape
    rows = height * width
    groups = gain_ref.shape[0]
    hid = b_in_ref.shape[1]
    n_z = n_dp // n_y
    n_x = n_chan // 2
    step = rows // chunks
    step_h = height // chunks
    me_dp = lax.axis_index("dp")
    me_z, me_y = lax.div(me_dp, n_y), lax.rem(me_dp, n_y)
    me_c = lax.axis_index("chan")
    me_x, core = lax.div(me_c, 2), lax.rem(me_c, 2)
    sib = me_x * 2 + (1 - core)
    sends = []

    def other(me, n, o):
        return lax.rem(me + o, n)

    def remote(src, dst, ss, rs, **device):
        return pltpu.make_async_remote_copy(
            src_ref=src, dst_ref=dst, send_sem=ss, recv_sem=rs,
            device_id=device, device_id_type=MESH,
        )

    def send(*args, **device):
        copy = remote(*args, **device)
        copy.start()
        sends.append(copy)

    loads = [
        pltpu.make_async_copy(a, b, in_sems.at[n])
        for n, (a, b) in enumerate(
            ((cot_hbm, cot_ref), (x_hbm, x_ref), (w_out_hbm, w_out), (w_in_hbm, w_in))
        )
    ]
    for load in loads:
        load.start()

    barrier = pltpu.get_barrier_semaphore()
    for o in range(1, n_chan):
        pl.semaphore_signal(
            barrier, inc=1, device_id={"chan": other(me_c, n_chan, o)}, device_id_type=MESH
        )
    for o in range(1, n_dp):
        pl.semaphore_signal(
            barrier, inc=1, device_id={"dp": other(me_dp, n_dp, o)}, device_id_type=MESH
        )
    pl.semaphore_wait(barrier, n_chan + n_dp - 2)

    def gather_start(buf, j, lo, size):
        part = buf.at[me_c, pl.ds(lo, size)]
        for o in range(1, n_x):
            q = other(me_x, n_x, o)
            send(part, part, ag_xs.at[o, j], ag_xr.at[me_x, j], chan=q * 2 + core)
        send(part, part, ag_ss.at[j], ag_sr.at[j], chan=sib)

    def gather_relay(buf, j, lo, size):
        for o in range(1, n_x):
            q = other(me_x, n_x, o)
            part = buf.at[q * 2 + core, pl.ds(lo, size)]
            remote(part, part, ag_xs.at[o, j], ag_xr.at[q, j], chan=q * 2 + core).wait_recv()
            send(part, part, ag_fs.at[o, j], ag_fr.at[q, j], chan=sib)

    def gather_wait(buf, j, lo, size):
        part = buf.at[sib, pl.ds(lo, size)]
        remote(part, part, ag_ss.at[j], ag_sr.at[j], chan=sib).wait_recv()
        for o in range(1, n_x):
            q = other(me_x, n_x, o)
            part = buf.at[q * 2 + 1 - core, pl.ds(lo, size)]
            remote(part, part, ag_fs.at[o, j], ag_fr.at[q, j], chan=sib).wait_recv()

    def moments_send(turn):
        for o in range(1, n_dp):
            d = other(me_dp, n_dp, o)
            send(
                mom_send.at[turn], mom_recv.at[turn, me_dp],
                mom_ss.at[turn, o], mom_sr.at[turn, me_dp], dp=d,
            )

    def moments_wait(turn):
        for o in range(1, n_dp):
            d = other(me_dp, n_dp, o)
            remote(
                mom_send.at[turn], mom_recv.at[turn, d],
                mom_ss.at[turn, o], mom_sr.at[turn, d], dp=d,
            ).wait_recv()

    def label_of(d):
        end = jnp.int32(0)
        label = jnp.int32(0)
        for g in range(groups):
            end = end + sizes_ref[g]
            label = label + (end <= d).astype(jnp.int32)
        return label

    mine = label_of(me_dp)
    count = jnp.float32(0)
    own_gain = jnp.zeros((1, channels), F32)
    own_bias = jnp.zeros((1, channels), F32)
    for g in range(groups):
        is_mine = (mine == g).astype(F32)
        count = count + is_mine * (sizes_ref[g] * rows).astype(F32)
        own_gain = own_gain + is_mine * gain_ref[g : g + 1]
        own_bias = own_bias + is_mine * bias_ref[g : g + 1]
    count = jnp.full((1, channels), count, F32)

    loads[0].wait()
    for i in range(chunks):
        lo = i * step
        cot = cot_ref[0, i * step_h : (i + 1) * step_h].reshape(step, channels)
        dfull[me_c, lo : lo + step] = (cot.astype(F32) * scale_ref[...]).astype(BF16)
    gather_start(dfull, chunks, 0, rows)

    loads[1].wait()

    def load_x(r):
        value = x_ref[0, r].astype(F32)
        source[r] = value
        return value

    fill_shifts(height, width, load_x, shifts)
    mom_send[0] = jnp.zeros(mom_send.shape[1:], F32)
    conv_forward(height, width, channels, shifts, taps_in, filt, mom_send.at[0])
    moments_send(0)
    gather_relay(dfull, chunks, 0, rows)
    loads[2].wait()
    moments_wait(0)
    mom_recv[0, me_dp] = mom_send[0]
    total = jnp.zeros(mom_send.shape[1:], F32)
    for d in range(n_dp):
        total = total + (label_of(d) == mine).astype(F32) * mom_recv[0, d]
    mean = total[0:1] / count
    rstd = lax.rsqrt(total[1:2] / count - mean * mean + EPS)

    for i in range(chunks):
        lo = i * step
        part = filt[i * step_h : (i + 1) * step_h].reshape(step, channels)
        centered = (part - mean) * rstd
        gath[me_c, lo : lo + step] = (centered * own_gain + own_bias).astype(BF16)
        gather_start(gath, i, lo, step)

    gather_wait(dfull, chunks, 0, rows)
    loads[3].wait()
    tile = 256

    def d_act_tile(n, carry):
        lo = pl.multiple_of(n * tile, tile)
        value = jnp.zeros((tile, hid), F32)
        for k in range(n_chan):
            value = value + lax.dot_general(
                dfull[k, pl.ds(lo, tile)], w_out[:, k * channels : (k + 1) * channels],
                CONTRACT_COLS, preferred_element_type=F32,
            )
        d_act[pl.ds(lo, tile)] = value
        return carry

    lax.fori_loop(0, rows // tile, d_act_tile, 0)
    bias_acc[...] = jnp.zeros(bias_acc.shape, F32)

    def hidden_chunk(lo):
        def one(n, carry):
            cols = pl.ds(pl.multiple_of(n * tile, tile), tile)
            value = jnp.zeros((step, tile), F32)
            for k in range(n_chan):
                value = value + jnp.dot(
                    gath[k, lo : lo + step], w_in[k * channels : (k + 1) * channels, cols],
                    preferred_element_type=F32,
                )
            value = value + b_in_ref[:, cols]
            out, slope = gelu_and_slope(value)
            act[lo : lo + step, cols] = out.astype(BF16)
            d_hid = d_act[lo : lo + step, cols] * slope
            bias_acc[0:1, cols] += jnp.sum(d_hid, axis=0, keepdims=True)
            hid_b[lo : lo + step, cols] = d_hid.astype(BF16)
            return carry

        lax.fori_loop(0, hid // tile, one, 0)

    def scatter_sibling(kind, i, product):
        lo = i * step
        for q in range(n_x):
            value = product(lo, q * 2 + 1 - core)
            sib_send[kind, i, q] = value.astype(BF16)
        send(
            sib_send.at[kind, i], sib_recv.at[kind, i],
            rs_ss.at[kind, i], rs_sr.at[kind, i], chan=sib,
        )
        for q in range(n_x):
            own_part[kind, q, lo : lo + step] = product(lo, q * 2 + core).astype(BF16)

    def scatter_chips(kind, i):
        lo = i * step
        remote(
            sib_send.at[kind, i], sib_recv.at[kind, i],
            rs_ss.at[kind, i], rs_sr.at[kind, i], chan=sib,
        ).wait_recv()
        for o in range(1, n_x):
            q = other(me_x, n_x, o)
            both = own_part[kind, q, lo : lo + step].astype(F32) + sib_recv[kind, i, q].astype(F32)
            x_send[kind, o, lo : lo + step] = both.astype(BF16)
            send(
                x_send.at[kind, o, pl.ds(lo, step)], x_recv.at[kind, me_x, pl.ds(lo, step)],
                rs_xs.at[kind, o, i], rs_xr.at[kind, me_x, i], chan=q * 2 + core,
            )

    def scatter_finish(kind, i):
        lo = i * step
        value = own_part[kind, me_x, lo : lo + step].astype(F32)
        value = value + sib_recv[kind, i, me_x].astype(F32)
        for o in range(1, n_x):
            q = other(me_x, n_x, o)
            remote(
                x_send.at[kind, o, pl.ds(lo, step)], x_recv.at[kind, q, pl.ds(lo, step)],
                rs_xs.at[kind, o, i], rs_xr.at[kind, q, i], chan=q * 2 + core,
            ).wait_recv()
            value = value + x_recv[kind, q, lo : lo + step].astype(F32)
        return value

    def normed_product(lo, k):
        weight = w_in[pl.ds(pl.multiple_of(k * channels, channels), channels), :]
        return lax.dot_general(
            hid_b[lo : lo + step], weight, CONTRACT_COLS, preferred_element_type=F32
        )

    def branch_product(lo, k):
        weight = w_out[:, pl.ds(pl.multiple_of(k * channels, channels), channels)]
        return jnp.dot(act[lo : lo + step], weight, preferred_element_type=F32)

    gather_relay(gath, 0, 0, step)
    for i in range(chunks):
        if i + 1 < chunks:
            gather_relay(gath, i + 1, (i + 1) * step, step)
        gather_wait(gath, i, i * step, step)
        hidden_chunk(i * step)
        scatter_sibling(0, i, normed_product)
        if i >= 1:
            scatter_chips(0, i - 1)
    scatter_chips(0, chunks - 1)

    part_rows = w_send.shape[2]
    per = channels // part_rows

    def weight_grad(t, left, right):
        for k in range(n_chan):
            value = lax.dot_general(
                left[k], right[...], CONTRACT_ROWS, preferred_element_type=F32
            ).astype(BF16)
            for j in range(per):
                d = k * per + j
                w_send[t, (d % n_y) * n_z + d // n_y] = value[j * part_rows : (j + 1) * part_rows]
        for o in range(1, n_y):
            y = other(me_y, n_y, o)
            send(
                w_send.at[t, pl.ds(y * n_z, n_z)], w_recv.at[t, me_y],
                wy_s.at[t, o], wy_r.at[t, me_y], dp=me_z * n_y + y,
            )

    weight_grad(1, dfull, act)
    weight_grad(0, gath, hid_b)

    for i in range(chunks):
        scatter_sibling(1, i, branch_product)
        if i >= 1:
            scatter_chips(1, i - 1)
    scatter_chips(1, chunks - 1)

    gain_term = jnp.zeros((1, channels), F32)
    bias_term = jnp.zeros((1, channels), F32)
    for i in range(chunks):
        value = scatter_finish(0, i)
        part = filt[i * step_h : (i + 1) * step_h].reshape(step, channels)
        centered = (part - mean) * rstd
        gain_term = gain_term + jnp.sum(value * centered, axis=0, keepdims=True)
        bias_term = bias_term + jnp.sum(value, axis=0, keepdims=True)
        dn[i * step_h : (i + 1) * step_h] = value.reshape(step_h, width, channels)
    mom_send[1] = jnp.zeros(mom_send.shape[1:], F32)
    mom_send[1, 0:1] = gain_term
    mom_send[1, 1:2] = bias_term
    moments_send(1)
    mom_recv[1, me_dp] = mom_send[1]
    moments_wait(1)
    group_sum = [jnp.zeros(mom_send.shape[1:], F32) for _ in range(groups)]
    for d in range(n_dp):
        value = mom_recv[1, d]
        label = label_of(d)
        for g in range(groups):
            group_sum[g] = group_sum[g] + (label == g).astype(F32) * value
    own_sum = jnp.zeros(mom_send.shape[1:], F32)
    for g in range(groups):
        dgain_ref[g : g + 1] = group_sum[g][0:1]
        dbias_ref[g : g + 1] = group_sum[g][1:2]
        own_sum = own_sum + (mine == g).astype(F32) * group_sum[g]
    mean_gain, mean_bias = own_sum[0:1] / count, own_sum[1:2] / count
    factor = own_gain * rstd

    def load_row(r):
        centered = (filt[r] - mean) * rstd
        return factor * (dn[r] - mean_bias - centered * mean_gain)

    fill_shifts(height, width, load_row, shifts)
    conv_backward(height, width, channels, shifts, source, taps_in, filt, tap_sums)

    def finish_row(r, carry):
        din_ref[0, r] = (cot_ref[0, r].astype(F32) + filt[r]).astype(BF16)
        return carry

    lax.fori_loop(0, height, finish_row, 0)

    scale_sum = jnp.zeros((1, channels), F32)
    for i in range(chunks):
        branch = scatter_finish(1, i)
        cot = cot_ref[0, i * step_h : (i + 1) * step_h].reshape(step, channels).astype(F32)
        plain = source[i * step_h : (i + 1) * step_h].reshape(step, channels)
        scale_sum = scale_sum + jnp.sum(cot * branch, axis=0, keepdims=True)
        value = (plain + scale_ref[...] * branch).astype(BF16)
        result_ref[0, i * step_h : (i + 1) * step_h] = value.reshape(step_h, width, channels)

    n_taps = KS * KS
    pieces = hid // channels
    pack_y[me_y] = jnp.zeros(pack_y.shape[1:], F32)
    for tap in range(n_taps):
        pack_y[me_y, tap : tap + 1] = jnp.sum(tap_sums[tap], axis=0, keepdims=True)
    pack_y[me_y, n_taps : n_taps + 1] = scale_sum
    for p in range(pieces):
        pack_y[me_y, n_taps + 1 + p : n_taps + 2 + p] = bias_acc[
            0:1, p * channels : (p + 1) * channels
        ]
    for o in range(1, n_y):
        y = other(me_y, n_y, o)
        send(
            pack_y.at[me_y], pack_y.at[me_y], py_s.at[o], py_r.at[me_y], dp=me_z * n_y + y
        )

    def weight_stage(t):
        for o in range(1, n_y):
            y = other(me_y, n_y, o)
            remote(
                w_send.at[t, pl.ds(y * n_z, n_z)], w_recv.at[t, y],
                wy_s.at[t, o], wy_r.at[t, y], dp=me_z * n_y + y,
            ).wait_recv()
        for o in range(n_z):
            z = other(me_z, n_z, o)
            value = w_send[t, me_y * n_z + z].astype(F32)
            for p in range(1, n_y):
                value = value + w_recv[t, other(me_y, n_y, p), z].astype(F32)
            z_send[t, o] = value.astype(BF16)
            if o:
                send(
                    z_send.at[t, o], z_recv.at[t, me_z],
                    wz_s.at[t, o], wz_r.at[t, me_z], dp=z * n_y + me_y,
                )

    weight_stage(1)
    for o in range(1, n_y):
        y = other(me_y, n_y, o)
        remote(
            pack_y.at[y], pack_y.at[y], py_s.at[o], py_r.at[y], dp=me_z * n_y + y
        ).wait_recv()
    pack = pack_y[0]
    for y in range(1, n_y):
        pack = pack + pack_y[y]
    pack_z[me_z] = pack
    for o in range(1, n_z):
        z = other(me_z, n_z, o)
        send(
            pack_z.at[me_z], pack_z.at[me_z], pz_s.at[o], pz_r.at[me_z], dp=z * n_y + me_y
        )
    weight_stage(0)

    for o in range(1, n_z):
        z = other(me_z, n_z, o)
        remote(
            pack_z.at[z], pack_z.at[z], pz_s.at[o], pz_r.at[z], dp=z * n_y + me_y
        ).wait_recv()
    pack = pack_z[0]
    for z in range(1, n_z):
        pack = pack + pack_z[z]
    dk_ref[...] = pack[:n_taps]
    dscale_ref[...] = pack[n_taps : n_taps + 1]
    for p in range(pieces):
        dbin_ref[0:1, p * channels : (p + 1) * channels] = pack[n_taps + 1 + p : n_taps + 2 + p]

    def weight_finish(t):
        value = z_send[t, 0].astype(F32)
        for o in range(1, n_z):
            z = other(me_z, n_z, o)
            remote(
                z_send.at[t, o], z_recv.at[t, z], wz_s.at[t, o], wz_r.at[t, z],
                dp=z * n_y + me_y,
            ).wait_recv()
            value = value + z_recv[t, z].astype(F32)
        return value

    dwout_ref[...] = weight_finish(1).T
    dwin_ref[...] = weight_finish(0)
    for copy in sends:
        copy.wait_send()


def body(n_dp, n_chan, activations, cotangent, dw_kernel, norm_gain, norm_bias, w_in, b_in, w_out,
         layer_scale, group_sizes):
    _, height, width, channels = activations.shape
    rows = height * width
    full = w_in.shape[0]
    hid = w_in.shape[1]
    groups = norm_gain.shape[0]
    chunks = 4
    n_x = n_chan // 2
    n_y = 1
    while n_dp % (2 * n_y) == 0 and 2 * (2 * n_y) ** 2 <= n_dp:
        n_y *= 2
    n_z = n_dp // n_y
    part = full // n_dp
    step = rows // chunks
    pack_rows = -(-(KS * KS + 1 + hid // channels) // 8) * 8
    vmem = pl.BlockSpec(memory_space=pltpu.VMEM)
    hbm = pl.BlockSpec(memory_space=pl.ANY)
    smem = pl.BlockSpec(memory_space=pltpu.SMEM)
    sds = jax.ShapeDtypeStruct
    dma = pltpu.SemaphoreType.DMA
    outs = pl.pallas_call(
        functools.partial(block_kernel, n_dp, n_y, n_chan, chunks),
        out_shape=(
            sds(activations.shape, BF16),
            sds(activations.shape, BF16),
            sds((KS * KS, channels), F32),
            sds((groups, channels), F32),
            sds((groups, channels), F32),
            sds((part, hid), F32),
            sds((1, hid), F32),
            sds((hid, part), F32),
            sds((1, channels), F32),
        ),
        in_specs=[smem, hbm, hbm, vmem, vmem, vmem, hbm, vmem, hbm, vmem],
        out_specs=(vmem,) * 9,
        scratch_shapes=[
            pltpu.VMEM(activations.shape, BF16),
            pltpu.VMEM(activations.shape, BF16),
            pltpu.VMEM(w_in.shape, BF16),
            pltpu.VMEM(w_out.shape, BF16),
            pltpu.VMEM((height, width, channels), F32),
            pltpu.VMEM((height, width, channels), F32),
            pltpu.VMEM((KS, height, width, channels), F32),
            pltpu.VMEM((KS * KS, SUB, channels), F32),
            pltpu.VMEM((n_chan, rows, channels), BF16),
            pltpu.VMEM((n_chan, rows, channels), BF16),
            pltpu.VMEM((rows, hid), F32),
            pltpu.VMEM((rows, hid), BF16),
            pltpu.VMEM((rows, hid), BF16),
            pltpu.VMEM((2, chunks, n_x, step, channels), BF16),
            pltpu.VMEM((2, chunks, n_x, step, channels), BF16),
            pltpu.VMEM((2, n_x, rows, channels), BF16),
            pltpu.VMEM((2, n_x, rows, channels), BF16),
            pltpu.VMEM((2, n_x, rows, channels), BF16),
            pltpu.VMEM((height, width, channels), F32),
            pltpu.VMEM((2, 8, channels), F32),
            pltpu.VMEM((2, n_dp, 8, channels), F32),
            pltpu.VMEM((2, n_dp, part, hid), BF16),
            pltpu.VMEM((2, n_y, n_z, part, hid), BF16),
            pltpu.VMEM((2, n_z, part, hid), BF16),
            pltpu.VMEM((2, n_z, part, hid), BF16),
            pltpu.VMEM((n_y, pack_rows, channels), F32),
            pltpu.VMEM((n_z, pack_rows, channels), F32),
            pltpu.VMEM((8, hid), F32),
            dma((4,)),
            dma((n_x, chunks + 1)),
            dma((n_x, chunks + 1)),
            dma((chunks + 1,)),
            dma((chunks + 1,)),
            dma((n_x, chunks + 1)),
            dma((n_x, chunks + 1)),
            dma((2, chunks)),
            dma((2, chunks)),
            dma((2, n_x, chunks)),
            dma((2, n_x, chunks)),
            dma((2, n_dp)),
            dma((2, n_dp)),
            dma((2, n_y)),
            dma((2, n_y)),
            dma((2, n_z)),
            dma((2, n_z)),
            dma((n_y,)),
            dma((n_y,)),
            dma((n_z,)),
            dma((n_z,)),
        ],
        compiler_params=pltpu.CompilerParams(
            collective_id=0, has_side_effects=True, vmem_limit_bytes=60 * 1024 * 1024
        ),
    )(
        group_sizes, activations, cotangent, dw_kernel, norm_gain, norm_bias, w_in,
        b_in[None], w_out, layer_scale[None],
    )
    result, d_input, d_kernel, d_gain, d_bias, d_w_in, d_b_in, d_w_out, d_scale = outs
    return (result, d_input, d_kernel, d_gain, d_bias, d_w_in, d_b_in[0], d_w_out, d_scale[0])


def solution(mesh):
    step = functools.partial(body, mesh.shape["dp"], mesh.shape["chan"])
    in_specs = (
        P("dp", None, None, "chan"),
        P("dp", None, None, "chan"),
        P(None, "chan"),
        P(None, "chan"),
        P(None, "chan"),
        P(None, "chan"),
        P("chan"),
        P("chan", None),
        P("chan"),
        P(),
    )
    out_specs = (
        P("dp", None, None, "chan"),
        P("dp", None, None, "chan"),
        P(None, "chan"),
        P(None, "chan"),
        P(None, "chan"),
        P("dp", "chan"),
        P("chan"),
        P("chan", "dp"),
        P("chan"),
    )
    return jax.shard_map(step, mesh=mesh, in_specs=in_specs, out_specs=out_specs, check_vma=False)
```

time: 287 us -> 161 us (0.56)
  Pallas kernels: 13.5 us -> 149 us
  waiting for transfers between devices: 102 us -> 0 us
  blocking collectives: 92 us -> 0 us
  matrix products: 27.7 us -> 0 us
  other arithmetic: 17.1 us -> 0 us
  between operations: 14 us -> 0.72 us
  local copies, waits for them, and re-layouts: 19.2 us -> 8.42 us
    pallas_call x2 -> x1, Pallas kernels: 13.5 us -> 149 us  [body(): pl.pallas_call(functools.partial(block_kernel, n_dp, n_y, n_chan, chunks)...]
    all_gather x2 -> x0, blocking collectives: 54.9 us -> none  [the longest x1 27.9 us: body(): per_device = lax.all_gather(moments[None], 'dp', axis=0, tiled=True)]
    reduce_scatter x2 -> x0, waiting for transfers between devices: 45.6 us -> none  [the longest x1 31.3 us: body(): lax.psum_scatter(partial_branch.astype(jnp.bfloat16), 'chan', scatter_dim...]
    all_gather x2 -> x0, waiting for transfers between devices: 45.2 us -> none  [the longest x1 22.9 us: body(): branch_full = lax.all_gather(d_branch, 'chan', axis=1, tiled=True)]
    psum x1 -> x0, blocking collectives: 37 us -> none  [body(): lax.psum((kernel_local, bias_local, scale_local), 'dp')]
    dot_general x6 -> x0, matrix products: 27.7 us -> none  [the longest x1 7.48 us: body(): lax.dot_general(branch_full, w_out, contract_cols, preferred_element_type...]
    unnamed x6 -> x0, waiting for transfers between devices: 11.6 us -> none
    unnamed x31 -> x23, local copies, waits for them, and re-layouts: 17.2 us -> 8.42 us
  transfers between devices with their start and end apart: 5 -> 0, of which waited for: 5 -> 0; matrix products, arithmetic and copies ran while one was open for 8% -> 0% of each run, Pallas kernels for 3% -> 0%
where the time goes in v2:
time: 161 us; the launch traced here: 158 us
  Pallas kernels  149 us (93%)
  local copies, waits for them, and re-layouts  8.42 us (5%)
    pallas_call x1, Pallas kernels, body(): pl.pallas_call(functools.partial(block_kernel, n_dp, n_y, n_chan, chunks)...  149 us
    unnamed x23, local copies, waits for them, and re-layouts  8.42 us

profile of v2, /device:TPU:0, one launch (start us, length us, event | category | flops | bytes accessed | tf_op | source)
XLA Modules:
  0.0 157.8 jit_solution(13372186292894918430)
XLA Ops:
  0.6 148.6 %shard_map.169 = (bf16[1,16,64,256]{3,2,1,0:T(8,128)(2,1)}, bf16[1,16,64,256]{3,2,1,0:T(8,128)(2,1)}, f32[49,256]{1,0:T(8,128)}, f32[4,256]{1,0:T(4,128)}, f32[4...) custom-call(s32[4]{0:T(128)} %sizes_ref.1, ...), custom_call_target="tpu_custom_call" | custom-call | tf_op jit(solution)/shard_map/pallas_call | solution.py:554
  149.3 0.0 copy-start.2
  149.3 0.0 copy-start.5
  149.3 0.0 copy-start.4
  149.3 0.0 copy-start.1
  149.3 0.0 copy-start.3
  149.3 0.0 copy-start
  149.3 0.0 copy-start.6
  149.4 2.0 %copy.28 = bf16[1,16,64,256]{3,2,1,0:T(8,128)(2,1)} copy(bf16[1,16,64,256]{3,2,1,0:T(8,128)(2,1)} %get-tuple-element.36) | data formatting | bytes 1048576
  151.3 1.9 %copy.29 = bf16[1,16,64,256]{3,2,1,0:T(8,128)(2,1)} copy(bf16[1,16,64,256]{3,2,1,0:T(8,128)(2,1)} %get-tuple-element.37) | data formatting | bytes 1048576
  153.2 0.0 copy-done.2
  153.2 0.6 copy.30
  153.8 0.0 copy-done.5
  153.8 0.6 copy.31
  154.4 0.0 copy-done.4
  154.4 0.6 copy.32
  155.0 0.0 copy-done.1
  155.0 0.8 copy.33
  155.8 0.0 copy-done.3
  155.8 0.6 copy.34
  156.4 0.0 copy-done
  156.4 0.8 copy.35
  157.2 0.0 copy-done.6
  157.2 0.6 copy.36
Async XLA Ops:
  149.3 3.9 %copy-start.2 = (f32[49,256]{1,0:T(8,128)S(1)}, f32[49,256]{1,0:T(8,128)}, u32[]{:S(2)}) copy-start(f32[49,256]{1,0:T(8,128)} %get-tuple-element.38) | copy-start | bytes 150532
  149.3 4.5 %copy-start.5 = (f32[4,256]{1,0:T(4,128)S(1)}, f32[4,256]{1,0:T(4,128)}, u32[]{:S(2)}) copy-start(f32[4,256]{1,0:T(4,128)} %get-tuple-element.39) | copy-start | bytes 12292
  149.3 5.1 %copy-start.4 = (f32[4,256]{1,0:T(4,128)S(1)}, f32[4,256]{1,0:T(4,128)}, u32[]{:S(2)}) copy-start(f32[4,256]{1,0:T(4,128)} %get-tuple-element.40) | copy-start | bytes 12292
  149.3 5.7 %copy-start.1 = (f32[128,1024]{1,0:T(8,128)S(1)}, f32[128,1024]{1,0:T(8,128)}, u32[]{:S(2)}) copy-start(f32[128,1024]{1,0:T(8,128)} %get-tuple-element.41) | copy-start | bytes 1572868
  149.3 6.5 %copy-start.3 = (f32[1,1024]{1,0:T(1,128)S(1)}, f32[1,1024]{1,0:T(1,128)}, u32[]{:S(2)}) copy-start(f32[1,1024]{1,0:T(1,128)} %get-tuple-element.24) | copy-start | bytes 12292
  149.3 7.1 %copy-start = (f32[1024,128]{1,0:T(8,128)S(1)}, f32[1024,128]{1,0:T(8,128)}, u32[]{:S(2)}) copy-start(f32[1024,128]{1,0:T(8,128)} %get-tuple-element.43) | copy-start | bytes 1572868
  149.3 7.9 %copy-start.6 = (f32[1,256]{1,0:T(1,128)S(1)}, f32[1,256]{1,0:T(1,128)}, u32[]{:S(2)}) copy-start(f32[1,256]{1,0:T(1,128)} %get-tuple-element.26) | copy-start | bytes 3076

commit v3 on v2

--- a/solution.py
+++ b/solution.py
@@ -64,8 +64,10 @@
         moments_ref[1:2, lanes] = jnp.sum(second, axis=0, keepdims=True)
 
 
-def conv_backward(rows, width, channels, shifts_ref, source_ref, kernel_ref, grad_ref, taps_ref):
-    for lb in range(channels // LANE):
+def conv_backward(
+    lane_blocks, rows, width, shifts_ref, source_ref, kernel_ref, grad_ref, taps_ref
+):
+    for lb in lane_blocks:
         lanes = slice(lb * LANE, (lb + 1) * LANE)
         taps_ref[:, :, lanes] = jnp.zeros((KS * KS, SUB, LANE), jnp.float32)
 
@@ -257,23 +259,7 @@
     moments_send(0)
     gather_relay(dfull, chunks, 0, rows)
     loads[2].wait()
-    moments_wait(0)
-    mom_recv[0, me_dp] = mom_send[0]
-    total = jnp.zeros(mom_send.shape[1:], F32)
-    for d in range(n_dp):
-        total = total + (label_of(d) == mine).astype(F32) * mom_recv[0, d]
-    mean = total[0:1] / count
-    rstd = lax.rsqrt(total[1:2] / count - mean * mean + EPS)
-
-    for i in range(chunks):
-        lo = i * step
-        part = filt[i * step_h : (i + 1) * step_h].reshape(step, channels)
-        centered = (part - mean) * rstd
-        gath[me_c, lo : lo + step] = (centered * own_gain + own_bias).astype(BF16)
-        gather_start(gath, i, lo, step)
-
     gather_wait(dfull, chunks, 0, rows)
-    loads[3].wait()
     tile = 256
 
     def d_act_tile(n, carry):
@@ -287,7 +273,25 @@
         d_act[pl.ds(lo, tile)] = value
         return carry
 
-    lax.fori_loop(0, rows // tile, d_act_tile, 0)
+    early = rows // tile // 2
+    lax.fori_loop(0, early, d_act_tile, 0)
+    moments_wait(0)
+    mom_recv[0, me_dp] = mom_send[0]
+    total = jnp.zeros(mom_send.shape[1:], F32)
+    for d in range(n_dp):
+        total = total + (label_of(d) == mine).astype(F32) * mom_recv[0, d]
+    mean = total[0:1] / count
+    rstd = lax.rsqrt(total[1:2] / count - mean * mean + EPS)
+
+    for i in range(chunks):
+        lo = i * step
+        part = filt[i * step_h : (i + 1) * step_h].reshape(step, channels)
+        centered = (part - mean) * rstd
+        gath[me_c, lo : lo + step] = (centered * own_gain + own_bias).astype(BF16)
+        gather_start(gath, i, lo, step)
+
+    lax.fori_loop(early, rows // tile, d_act_tile, 0)
+    loads[3].wait()
     bias_acc[...] = jnp.zeros(bias_acc.shape, F32)
 
     def hidden_chunk(lo):
@@ -365,37 +369,70 @@
             gather_relay(gath, i + 1, (i + 1) * step, step)
         gather_wait(gath, i, i * step, step)
         hidden_chunk(i * step)
+
+    part_rows = w_send.shape[2]
+    per = channels // part_rows
+
+    order = [o % n_z for o in range(1, n_z + 1)]
+
+    def weight_block(t, left, right, k):
+        value = lax.dot_general(
+            left[k], right[...], CONTRACT_ROWS, preferred_element_type=F32
+        ).astype(BF16)
+        for j in range(per):
+            d = k * per + j
+            slot = lax.rem(d, n_y) * n_z + lax.div(d, n_y)
+            w_send[t, slot] = value[j * part_rows : (j + 1) * part_rows]
+
+    def weight_copy(t, o, p):
+        y, z = other(me_y, n_y, p), other(me_z, n_z, o)
+        return (
+            w_send.at[t, y * n_z + z], w_recv.at[t, me_y, z],
+            wy_s.at[t, p, o], wy_r.at[t, me_y, z],
+        ), me_z * n_y + y
+
+    def weight_issue(t, o):
+        for p in range(1, n_y):
+            args, d = weight_copy(t, o, p)
+            send(*args, dp=d)
+
+    def weight_grad(t, left, right, issue):
+        if per == n_y:
+            for o in order:
+                weight_block(t, left, right, other(me_z, n_z, o))
+                if issue:
+                    weight_issue(t, o)
+        else:
+            for k in range(n_chan):
+                weight_block(t, left, right, jnp.int32(k))
+            if issue:
+                for o in order:
+                    weight_issue(t, o)
+
+    def weight_stage(t, o):
+        z = other(me_z, n_z, o)
+        value = w_send[t, me_y * n_z + z].astype(F32)
+        for p in range(1, n_y):
+            y = other(me_y, n_y, p)
+            remote(
+                w_send.at[t, y * n_z + z], w_recv.at[t, y, z],
+                wy_s.at[t, p, o], wy_r.at[t, y, z], dp=me_z * n_y + y,
+            ).wait_recv()
+            value = value + w_recv[t, y, z].astype(F32)
+        z_send[t, o] = value.astype(BF16)
+        if o:
+            send(
+                z_send.at[t, o], z_recv.at[t, me_z],
+                wz_s.at[t, o], wz_r.at[t, me_z], dp=z * n_y + me_y,
+            )
+
+    weight_grad(1, dfull, act, True)
+    for i in range(chunks):
         scatter_sibling(0, i, normed_product)
         if i >= 1:
             scatter_chips(0, i - 1)
     scatter_chips(0, chunks - 1)
-
-    part_rows = w_send.shape[2]
-    per = channels // part_rows
-
-    def weight_grad(t, left, right):
-        for k in range(n_chan):
-            value = lax.dot_general(
-                left[k], right[...], CONTRACT_ROWS, preferred_element_type=F32
-            ).astype(BF16)
-            for j in range(per):
-                d = k * per + j
-                w_send[t, (d % n_y) * n_z + d // n_y] = value[j * part_rows : (j + 1) * part_rows]
-        for o in range(1, n_y):
-            y = other(me_y, n_y, o)
-            send(
-                w_send.at[t, pl.ds(y * n_z, n_z)], w_recv.at[t, me_y],
-                wy_s.at[t, o], wy_r.at[t, me_y], dp=me_z * n_y + y,
-            )
-
-    weight_grad(1, dfull, act)
-    weight_grad(0, gath, hid_b)
-
-    for i in range(chunks):
-        scatter_sibling(1, i, branch_product)
-        if i >= 1:
-            scatter_chips(1, i - 1)
-    scatter_chips(1, chunks - 1)
+    weight_grad(0, gath, hid_b, False)
 
     gain_term = jnp.zeros((1, channels), F32)
     bias_term = jnp.zeros((1, channels), F32)
@@ -411,6 +448,15 @@
     mom_send[1, 1:2] = bias_term
     moments_send(1)
     mom_recv[1, me_dp] = mom_send[1]
+    for o in order:
+        weight_issue(0, o)
+    for i in range(chunks):
+        scatter_sibling(1, i, branch_product)
+        if i >= 1:
+            scatter_chips(1, i - 1)
+    scatter_chips(1, chunks - 1)
+    for o in order:
+        weight_stage(1, o)
     moments_wait(1)
     group_sum = [jnp.zeros(mom_send.shape[1:], F32) for _ in range(groups)]
     for d in range(n_dp):
@@ -431,7 +477,12 @@
         return factor * (dn[r] - mean_bias - centered * mean_gain)
 
     fill_shifts(height, width, load_row, shifts)
-    conv_backward(height, width, channels, shifts, source, taps_in, filt, tap_sums)
+    lane_blocks = list(range(channels // LANE))
+    ready = list(order)
+    for lb in lane_blocks:
+        conv_backward([lb], height, width, shifts, source, taps_in, filt, tap_sums)
+        if len(ready) > 2:
+            weight_stage(0, ready.pop(0))
 
     def finish_row(r, carry):
         din_ref[0, r] = (cot_ref[0, r].astype(F32) + filt[r]).astype(BF16)
@@ -464,26 +515,8 @@
             pack_y.at[me_y], pack_y.at[me_y], py_s.at[o], py_r.at[me_y], dp=me_z * n_y + y
         )
 
-    def weight_stage(t):
-        for o in range(1, n_y):
-            y = other(me_y, n_y, o)
-            remote(
-                w_send.at[t, pl.ds(y * n_z, n_z)], w_recv.at[t, y],
-                wy_s.at[t, o], wy_r.at[t, y], dp=me_z * n_y + y,
-            ).wait_recv()
-        for o in range(n_z):
-            z = other(me_z, n_z, o)
-            value = w_send[t, me_y * n_z + z].astype(F32)
-            for p in range(1, n_y):
-                value = value + w_recv[t, other(me_y, n_y, p), z].astype(F32)
-            z_send[t, o] = value.astype(BF16)
-            if o:
-                send(
-                    z_send.at[t, o], z_recv.at[t, me_z],
-                    wz_s.at[t, o], wz_r.at[t, me_z], dp=z * n_y + me_y,
-                )
-
-    weight_stage(1)
+    while len(ready) > 1:
+        weight_stage(0, ready.pop(0))
     for o in range(1, n_y):
         y = other(me_y, n_y, o)
         remote(
@@ -498,7 +531,8 @@
         send(
             pack_z.at[me_z], pack_z.at[me_z], pz_s.at[o], pz_r.at[me_z], dp=z * n_y + me_y
         )
-    weight_stage(0)
+    for o in ready:
+        weight_stage(0, o)
 
     for o in range(1, n_z):
         z = other(me_z, n_z, o)
@@ -608,8 +642,8 @@
             dma((2, n_x, chunks)),
             dma((2, n_dp)),
             dma((2, n_dp)),
-            dma((2, n_y)),
-            dma((2, n_y)),
+            dma((2, n_y, n_z)),
+            dma((2, n_y, n_z)),
             dma((2, n_z)),
             dma((2, n_z)),
             dma((n_y,)),

time: 161 us -> 126 us (0.78); the launches traced: 158 us -> 126 us
  Pallas kernels: 149 us -> 117 us
    pallas_call x1, Pallas kernels: 149 us -> 117 us  [body(): pl.pallas_call(functools.partial(block_kernel, n_dp, n_y, n_chan, chunks)...]
where the time goes in v3:
time: 126 us
  Pallas kernels  117 us (93%)
  local copies, waits for them, and re-layouts  8.42 us (7%)
    pallas_call x1, Pallas kernels, body(): pl.pallas_call(functools.partial(block_kernel, n_dp, n_y, n_chan, chunks)...  117 us
    unnamed x23, local copies, waits for them, and re-layouts  8.42 us

profile of v3, /device:TPU:0, one launch (start us, length us, event | category | flops | bytes accessed | tf_op | source)
XLA Modules:
  0.0 125.7 jit_solution(17715919582690306325)
XLA Ops:
  0.6 116.6 %shard_map.169 = (bf16[1,16,64,256]{3,2,1,0:T(8,128)(2,1)}, bf16[1,16,64,256]{3,2,1,0:T(8,128)(2,1)}, f32[49,256]{1,0:T(8,128)}, f32[4,256]{1,0:T(4,128)}, f32[4...) custom-call(s32[4]{0:T(128)} %sizes_ref.1, ...), custom_call_target="tpu_custom_call" | custom-call | tf_op jit(solution)/shard_map/pallas_call | solution.py:588
  117.2 0.0 copy-start.2
  117.2 0.0 copy-start.5
  117.3 0.0 copy-start.4
  117.3 0.0 copy-start.1
  117.3 0.0 copy-start.3
  117.3 0.0 copy-start
  117.3 0.0 copy-start.6
  117.3 2.0 %copy.28 = bf16[1,16,64,256]{3,2,1,0:T(8,128)(2,1)} copy(bf16[1,16,64,256]{3,2,1,0:T(8,128)(2,1)} %get-tuple-element.36) | data formatting | bytes 1048576
  119.3 1.9 %copy.29 = bf16[1,16,64,256]{3,2,1,0:T(8,128)(2,1)} copy(bf16[1,16,64,256]{3,2,1,0:T(8,128)(2,1)} %get-tuple-element.37) | data formatting | bytes 1048576
  121.2 0.0 copy-done.2
  121.2 0.6 copy.30
  121.8 0.0 copy-done.5
  121.8 0.6 copy.31
  122.4 0.0 copy-done.4
  122.4 0.6 copy.32
  123.0 0.0 copy-done.1
  123.0 0.8 copy.33
  123.8 0.0 copy-done.3
  123.8 0.6 copy.34
  124.4 0.0 copy-done
  124.4 0.8 copy.35
  125.2 0.0 copy-done.6
  125.2 0.6 copy.36
Async XLA Ops:
  117.2 3.9 %copy-start.2 = (f32[49,256]{1,0:T(8,128)S(1)}, f32[49,256]{1,0:T(8,128)}, u32[]{:S(2)}) copy-start(f32[49,256]{1,0:T(8,128)} %get-tuple-element.38) | copy-start | bytes 150532
  117.2 4.5 %copy-start.5 = (f32[4,256]{1,0:T(4,128)S(1)}, f32[4,256]{1,0:T(4,128)}, u32[]{:S(2)}) copy-start(f32[4,256]{1,0:T(4,128)} %get-tuple-element.39) | copy-start | bytes 12292
  117.3 5.1 %copy-start.4 = (f32[4,256]{1,0:T(4,128)S(1)}, f32[4,256]{1,0:T(4,128)}, u32[]{:S(2)}) copy-start(f32[4,256]{1,0:T(4,128)} %get-tuple-element.40) | copy-start | bytes 12292
  117.3 5.7 %copy-start.1 = (f32[128,1024]{1,0:T(8,128)S(1)}, f32[128,1024]{1,0:T(8,128)}, u32[]{:S(2)}) copy-start(f32[128,1024]{1,0:T(8,128)} %get-tuple-element.41) | copy-start | bytes 1572868
  117.3 6.5 %copy-start.3 = (f32[1,1024]{1,0:T(1,128)S(1)}, f32[1,1024]{1,0:T(1,128)}, u32[]{:S(2)}) copy-start(f32[1,1024]{1,0:T(1,128)} %get-tuple-element.24) | copy-start | bytes 12292
  117.3 7.1 %copy-start = (f32[1024,128]{1,0:T(8,128)S(1)}, f32[1024,128]{1,0:T(8,128)}, u32[]{:S(2)}) copy-start(f32[1024,128]{1,0:T(8,128)} %get-tuple-element.43) | copy-start | bytes 1572868
  117.3 7.9 %copy-start.6 = (f32[1,256]{1,0:T(1,128)S(1)}, f32[1,256]{1,0:T(1,128)}, u32[]{:S(2)}) copy-start(f32[1,256]{1,0:T(1,128)} %get-tuple-element.26) | copy-start | bytes 3076
